TPU v7x, 32 devices: a whole 2x2x4 slice. The times are simulated.
32 devices in a mesh: ctx: 8 (over z, core), fsdp: 4 (over y, x).
Axes of the slice: x: 2, y: 2, z: 4, core: 2. Of those that a mesh axis runs over, the one named last changes fastest.
Arguments:
- block_input: bfloat16 [2, 4, 2048, 767], P(None, 'fsdp', 'ctx'), may hold values from -6 to 6
- cotangent: bfloat16 [2, 4, 2048, 767], P(None, 'fsdp', 'ctx'), may hold values from -6 to 6
- segment_ids: int32 [2, 4, 2048], P(None, 'fsdp'), may hold values from 0 to 7, never falling along the last dimension, each value on 1 to 512 neighbouring positions
- block_order: int32 [16], replicated, may hold values from 0 to 15, as said below
- gain_attn: bfloat16 [2, 768], P(None, 'fsdp'), may hold values from 0.5 to 1.5
- w_qkv: bfloat16 [2, 768, 2304], P(None, 'fsdp'), may hold values from -0.21875 to 0.21875
- bias_q: bfloat16 [2, 768], P(None, 'fsdp'), may hold values from -3 to 3
- bias_v: bfloat16 [2, 768], P(None, 'fsdp'), may hold values from -3 to 3
- w_out: bfloat16 [2, 768, 768], P(None, 'fsdp'), may hold values from -1.75 to 1.75
- bias_out: bfloat16 [2, 768], P(None, 'fsdp'), may hold values from -3 to 3
- gain_mlp: bfloat16 [2, 768], P(None, 'fsdp'), may hold values from 0.5 to 1.5
- w_up: bfloat16 [2, 768, 3072], P(None, 'fsdp'), may hold values from -0.21875 to 0.21875
- bias_up: bfloat16 [2, 3072], P(None, 'fsdp'), may hold values from -3 to 3
- w_down: bfloat16 [2, 3072, 768], P(None, 'fsdp'), may hold values from -0.109375 to 0.109375
- bias_down: bfloat16 [2, 768], P(None, 'fsdp'), may hold values from -3 to 3
Outputs:
- block_output: bfloat16 [2, 4, 2048, 767], P(None, 'fsdp', 'ctx')
- grad_input: float32 [2, 4, 2048, 767], P(None, 'fsdp', 'ctx')
- grad_gain_attn: float32 [2, 768], P(None, 'fsdp')
- grad_w_qkv: float32 [2, 768, 2304], P(None, 'fsdp')
- grad_bias_q: float32 [2, 768], P(None, 'fsdp')
- grad_bias_v: float32 [2, 768], P(None, 'fsdp')
- grad_w_out: float32 [2, 768, 768], P(None, 'fsdp')
- grad_bias_out: float32 [2, 768], P(None, 'fsdp')
- grad_gain_mlp: float32 [2, 768], P(None, 'fsdp')
- grad_w_up: float32 [2, 768, 3072], P(None, 'fsdp')
- grad_bias_up: float32 [2, 3072], P(None, 'fsdp')
- grad_w_down: float32 [2, 3072, 768], P(None, 'fsdp')
- grad_bias_down: float32 [2, 768], P(None, 'fsdp')
Inputs may be any that keep to these rules, and one draw needn't show every extreme that they name: `block_order`: entries 2c and 2c + 1 hold blocks p and 15 - p of the sequence for some p, the lower first; each block appears once. `segment_ids`: along each sequence the document numbers never fall and each of the 8 documents holds 1 to 512 tokens, one exactly 512.
All inputs are finite; a program needn't handle non-finite values.
Results may differ from a plain program's by a relative error of at most 0.022.
Values may be sent and summed in bfloat16 or wider, within the bound.
A program may use at most 384 MiB of HBM per device.

v0:
```python
from functools import partial

import jax
import jax.numpy as jnp
from jax import lax
from jax.sharding import PartitionSpec as P

HD = 64


eps = 1e-06
negative = -1e30


def normed(hidden, gain):
    full = jnp.concatenate([hidden, -jnp.sum(hidden, axis=-1, keepdims=True)], axis=-1)
    return full * lax.rsqrt(jnp.mean(full * full, axis=-1, keepdims=True) + eps) * gain


def compress(branch):
    return (branch - jnp.mean(branch, axis=-1, keepdims=True))[..., :-1]


def expand_grad(grad_rows):
    padded = jnp.concatenate([grad_rows, jnp.zeros_like(grad_rows[..., :1])], axis=-1)
    return padded - jnp.mean(padded, axis=-1, keepdims=True)


def fetch_layer(weights, layer_index):
    return (
        lax.all_gather(weights[0][layer_index], "fsdp", axis=0, tiled=True),
        lax.all_gather(weights[1][layer_index], "fsdp", axis=0, tiled=True),
        lax.all_gather(weights[2][layer_index], "fsdp", axis=0, tiled=True),
        lax.all_gather(weights[3][layer_index], "fsdp", axis=0, tiled=True),
        lax.all_gather(weights[4][layer_index], "fsdp", axis=0, tiled=True),
        lax.all_gather(weights[5][layer_index], "fsdp", axis=0, tiled=True),
        lax.all_gather(weights[6][layer_index], "fsdp", axis=0, tiled=True),
        lax.all_gather(weights[7][layer_index], "fsdp", axis=0, tiled=True),
        lax.all_gather(weights[8][layer_index], "fsdp", axis=0, tiled=True),
        lax.all_gather(weights[9][layer_index], "fsdp", axis=0, tiled=True),
        lax.all_gather(weights[10][layer_index], "fsdp", axis=0, tiled=True),
    )


def fetch_again(weights, layer_index):
    return (
        lax.all_gather(weights[0][layer_index], "fsdp", axis=0, tiled=True),
        lax.all_gather(weights[1][layer_index], "fsdp", axis=0, tiled=True),
        lax.all_gather(weights[2][layer_index], "fsdp", axis=0, tiled=True),
        lax.all_gather(weights[3][layer_index], "fsdp", axis=0, tiled=True),
        lax.all_gather(weights[4][layer_index], "fsdp", axis=0, tiled=True),
        lax.all_gather(weights[5][layer_index], "fsdp", axis=0, tiled=True),
        lax.all_gather(weights[6][layer_index], "fsdp", axis=0, tiled=True),
        lax.all_gather(weights[7][layer_index], "fsdp", axis=0, tiled=True),
        lax.all_gather(weights[8][layer_index], "fsdp", axis=0, tiled=True),
        lax.all_gather(weights[9][layer_index], "fsdp", axis=0, tiled=True),
        lax.all_gather(weights[10][layer_index], "fsdp", axis=0, tiled=True),
    )


def scatter_gradients(grads):
    return (
        lax.psum_scatter(
            grads[0].astype(jnp.bfloat16), "fsdp", scatter_dimension=0, tiled=True
        ).astype(jnp.float32),
        lax.psum_scatter(
            grads[1].astype(jnp.bfloat16), "fsdp", scatter_dimension=0, tiled=True
        ).astype(jnp.float32),
        lax.psum_scatter(
            grads[2].astype(jnp.bfloat16), "fsdp", scatter_dimension=0, tiled=True
        ).astype(jnp.float32),
        lax.psum_scatter(
            grads[3].astype(jnp.bfloat16), "fsdp", scatter_dimension=0, tiled=True
        ).astype(jnp.float32),
        lax.psum_scatter(
            grads[4].astype(jnp.bfloat16), "fsdp", scatter_dimension=0, tiled=True
        ).astype(jnp.float32),
        lax.psum_scatter(
            grads[5].astype(jnp.bfloat16), "fsdp", scatter_dimension=0, tiled=True
        ).astype(jnp.float32),
        lax.psum_scatter(
            grads[6].astype(jnp.bfloat16), "fsdp", scatter_dimension=0, tiled=True
        ).astype(jnp.float32),
        lax.psum_scatter(
            grads[7].astype(jnp.bfloat16), "fsdp", scatter_dimension=0, tiled=True
        ).astype(jnp.float32),
        lax.psum_scatter(
            grads[8].astype(jnp.bfloat16), "fsdp", scatter_dimension=0, tiled=True
        ).astype(jnp.float32),
        lax.psum_scatter(
            grads[9].astype(jnp.bfloat16), "fsdp", scatter_dimension=0, tiled=True
        ).astype(jnp.float32),
        lax.psum_scatter(
            grads[10].astype(jnp.bfloat16), "fsdp", scatter_dimension=0, tiled=True
        ).astype(jnp.float32),
    )


def total_gradients(grads):
    return (
        lax.psum(grads[0].astype(jnp.bfloat16), "ctx").astype(jnp.float32),
        lax.psum(grads[1].astype(jnp.bfloat16), "ctx").astype(jnp.float32),
        lax.psum(grads[2].astype(jnp.bfloat16), "ctx").astype(jnp.float32),
        lax.psum(grads[3].astype(jnp.bfloat16), "ctx").astype(jnp.float32),
        lax.psum(grads[4].astype(jnp.bfloat16), "ctx").astype(jnp.float32),
        lax.psum(grads[5].astype(jnp.bfloat16), "ctx").astype(jnp.float32),
        lax.psum(grads[6].astype(jnp.bfloat16), "ctx").astype(jnp.float32),
        lax.psum(grads[7].astype(jnp.bfloat16), "ctx").astype(jnp.float32),
        lax.psum(grads[8].astype(jnp.bfloat16), "ctx").astype(jnp.float32),
        lax.psum(grads[9].astype(jnp.bfloat16), "ctx").astype(jnp.float32),
        lax.psum(grads[10].astype(jnp.bfloat16), "ctx").astype(jnp.float32),
    )


def pair_slice(matrix, pair_index, head_dim):
    piece = lax.dynamic_slice_in_dim(matrix, pair_index * 2 * head_dim, 2 * head_dim, 2)
    return piece.reshape(matrix.shape[0], matrix.shape[1], 2, head_dim)


def join_pairs(stacked):
    pair_count, seq_count, row_count, pair_width = stacked.shape
    return stacked.transpose(1, 2, 0, 3).reshape(seq_count, row_count, pair_count * pair_width)


def attend_forward(queries, keys_all, values_all, allowed, head_dim):
    pair_count = queries.shape[2] // (2 * head_dim)
    score_scale = head_dim ** (-0.5)

    def one_pair(pair_index):
        query_pair = pair_slice(queries, pair_index, head_dim)
        key_pair = pair_slice(keys_all, pair_index, head_dim)
        value_pair = pair_slice(values_all, pair_index, head_dim)
        raw_scores = jnp.einsum(
            "sqgd,skgd->sgqk", query_pair, key_pair, preferred_element_type=jnp.float32
        )
        scaled = jnp.where(allowed[:, None], raw_scores * score_scale, negative)
        row_max = jnp.max(scaled, axis=-1, keepdims=True)
        exp_scores = jnp.exp(scaled - row_max)
        row_total = jnp.sum(exp_scores, axis=-1, keepdims=True)
        soft_probs = (exp_scores / row_total).astype(jnp.bfloat16)
        pair_mixed = jnp.einsum(
            "sgqk,skgd->sqgd", soft_probs, value_pair, preferred_element_type=jnp.float32
        )
        pair_mixed = pair_mixed.astype(jnp.bfloat16).reshape(
            queries.shape[0], queries.shape[1], 2 * head_dim
        )
        return (pair_mixed, (row_max + jnp.log(row_total))[..., 0])

    stacked, logsum = lax.map(one_pair, jnp.arange(pair_count, dtype=jnp.int32))
    return (join_pairs(stacked), logsum)


def attend_backward(queries, keys_all, values_all, allowed, logsum, grad_mixed, head_dim):
    pair_count = queries.shape[2] // (2 * head_dim)
    score_scale = head_dim ** (-0.5)

    def one_pair(pair_item):
        pair_index, pair_logsum = pair_item
        query_pair = pair_slice(queries, pair_index, head_dim)
        key_pair = pair_slice(keys_all, pair_index, head_dim)
        value_pair = pair_slice(values_all, pair_index, head_dim)
        grad_pair = pair_slice(grad_mixed, pair_index, head_dim)
        raw_scores = jnp.einsum(
            "sqgd,skgd->sgqk", query_pair, key_pair, preferred_element_type=jnp.float32
        )
        scaled = jnp.where(allowed[:, None], raw_scores * score_scale, negative)
        soft_probs = jnp.exp(scaled - pair_logsum[..., None])
        grad_probs = jnp.einsum(
            "sqgd,skgd->sgqk", grad_pair, value_pair, preferred_element_type=jnp.float32
        )
        inner = jnp.sum(grad_probs * soft_probs, axis=-1, keepdims=True)
        grad_raw = (soft_probs * (grad_probs - inner) * score_scale).astype(jnp.bfloat16)
        grad_query = jnp.einsum(
            "sgqk,skgd->sqgd", grad_raw, key_pair, preferred_element_type=jnp.float32
        )
        grad_key = jnp.einsum(
            "sgqk,sqgd->skgd", grad_raw, query_pair, preferred_element_type=jnp.float32
        )
        grad_value = jnp.einsum(
            "sgqk,sqgd->skgd",
            soft_probs.astype(jnp.bfloat16),
            grad_pair,
            preferred_element_type=jnp.float32,
        )
        seq_count, row_count = (queries.shape[0], queries.shape[1])
        key_count = keys_all.shape[1]
        return (
            grad_query.astype(jnp.bfloat16).reshape(seq_count, row_count, 2 * head_dim),
            grad_key.reshape(seq_count, key_count, 2 * head_dim),
            grad_value.reshape(seq_count, key_count, 2 * head_dim),
        )

    grad_query, grad_key, grad_value = lax.map(
        one_pair, (jnp.arange(pair_count, dtype=jnp.int32), logsum)
    )
    return (join_pairs(grad_query), join_pairs(grad_key), join_pairs(grad_value))


def layer_forward(hidden, layer_weights, allowed, head_dim):
    (
        gain_attn,
        w_qkv,
        bias_q,
        bias_v,
        w_out,
        bias_out,
        gain_mlp,
        w_up,
        bias_up,
        w_down,
        bias_down,
    ) = layer_weights
    model_width = w_out.shape[0]
    normed_attn = normed(hidden, gain_attn.astype(jnp.float32)).astype(jnp.bfloat16)
    projected = jnp.einsum("srd,de->sre", normed_attn, w_qkv, preferred_element_type=jnp.float32)
    queries = (projected[..., :model_width] + bias_q.astype(jnp.float32)).astype(jnp.bfloat16)
    key_rows = projected[..., model_width : 2 * model_width].astype(jnp.bfloat16)
    values = (projected[..., 2 * model_width :] + bias_v.astype(jnp.float32)).astype(jnp.bfloat16)
    keys_all, values_all = (
        lax.all_gather(key_rows, "ctx", axis=1, tiled=True),
        lax.all_gather(values, "ctx", axis=1, tiled=True),
    )
    attn_mixed, logsum = attend_forward(queries, keys_all, values_all, allowed, head_dim)
    attn_branch = jnp.einsum(
        "srd,de->sre", attn_mixed, w_out, preferred_element_type=jnp.float32
    ) + bias_out.astype(jnp.float32)
    middle = hidden + compress(attn_branch)
    normed_mlp = normed(middle, gain_mlp.astype(jnp.float32)).astype(jnp.bfloat16)
    preact = jnp.einsum(
        "srd,df->srf", normed_mlp, w_up, preferred_element_type=jnp.float32
    ) + bias_up.astype(jnp.float32)
    activated = jax.nn.gelu(preact, approximate=True).astype(jnp.bfloat16)
    mlp_branch = jnp.einsum(
        "srf,fd->srd", activated, w_down, preferred_element_type=jnp.float32
    ) + bias_down.astype(jnp.float32)
    kept_values = (
        hidden,
        normed_attn,
        queries,
        key_rows,
        values,
        keys_all,
        values_all,
        attn_mixed,
        logsum,
        middle,
        normed_mlp,
        preact,
        activated,
    )
    return (middle + compress(mlp_branch), kept_values)


def column_sums(matrix):
    return jnp.sum(matrix.astype(jnp.float32), axis=(0, 1))


def layer_backward(grad_after, kept_values, layer_weights, allowed, head_dim):
    (
        gain_attn,
        w_qkv,
        bias_q,
        bias_v,
        w_out,
        bias_out,
        gain_mlp,
        w_up,
        bias_up,
        w_down,
        bias_down,
    ) = layer_weights
    (
        hidden,
        normed_attn,
        queries,
        key_rows,
        values,
        keys_all,
        values_all,
        attn_mixed,
        logsum,
        middle,
        normed_mlp,
        preact,
        activated,
    ) = kept_values
    grad_mlp_branch = expand_grad(grad_after).astype(jnp.bfloat16)
    grad_w_down = jnp.einsum(
        "srf,srd->fd", activated, grad_mlp_branch, preferred_element_type=jnp.float32
    )
    grad_bias_down = column_sums(grad_mlp_branch)
    grad_activated = jnp.einsum(
        "srd,fd->srf", grad_mlp_branch, w_down, preferred_element_type=jnp.float32
    )
    gelu_pull = jax.vjp(partial(jax.nn.gelu, approximate=True), preact)[1]
    grad_preact = gelu_pull(grad_activated)[0].astype(jnp.bfloat16)
    grad_w_up = jnp.einsum(
        "srd,srf->df", normed_mlp, grad_preact, preferred_element_type=jnp.float32
    )
    grad_bias_up = column_sums(grad_preact)
    grad_normed_mlp = jnp.einsum(
        "srf,df->srd", grad_preact, w_up, preferred_element_type=jnp.float32
    )
    mlp_pull = jax.vjp(normed, middle, gain_mlp.astype(jnp.float32))[1]
    grad_middle_norm, grad_gain_mlp = mlp_pull(grad_normed_mlp)
    grad_middle = grad_after + grad_middle_norm
    grad_attn_branch = expand_grad(grad_middle).astype(jnp.bfloat16)
    grad_w_out = jnp.einsum(
        "srd,sre->de", attn_mixed, grad_attn_branch, preferred_element_type=jnp.float32
    )
    grad_bias_out = column_sums(grad_attn_branch)
    grad_mixed = jnp.einsum(
        "sre,de->srd", grad_attn_branch, w_out, preferred_element_type=jnp.float32
    ).astype(jnp.bfloat16)
    grad_queries, grad_keys_all, grad_values_all = attend_backward(
        queries, keys_all, values_all, allowed, logsum, grad_mixed, head_dim
    )
    grad_keys, grad_values = (
        lax.psum_scatter(
            grad_keys_all.astype(jnp.bfloat16), "ctx", scatter_dimension=1, tiled=True
        ).astype(jnp.float32),
        lax.psum_scatter(
            grad_values_all.astype(jnp.bfloat16), "ctx", scatter_dimension=1, tiled=True
        ).astype(jnp.float32),
    )
    grad_keys = grad_keys.astype(jnp.bfloat16)
    grad_values = grad_values.astype(jnp.bfloat16)
    grad_projected = jnp.concatenate([grad_queries, grad_keys, grad_values], axis=-1)
    grad_w_qkv = jnp.einsum(
        "srd,sre->de", normed_attn, grad_projected, preferred_element_type=jnp.float32
    )
    grad_bias_q = column_sums(grad_queries)
    grad_bias_v = column_sums(grad_values)
    grad_normed_attn = jnp.einsum(
        "sre,de->srd", grad_projected, w_qkv, preferred_element_type=jnp.float32
    )
    attn_pull = jax.vjp(normed, hidden, gain_attn.astype(jnp.float32))[1]
    grad_hidden_norm, grad_gain_attn = attn_pull(grad_normed_attn)
    layer_grads = (
        grad_gain_attn,
        grad_w_qkv,
        grad_bias_q,
        grad_bias_v,
        grad_w_out,
        grad_bias_out,
        grad_gain_mlp,
        grad_w_up,
        grad_bias_up,
        grad_w_down,
        grad_bias_down,
    )
    return (grad_middle + grad_hidden_norm, layer_grads)


def shards(
    block_input,
    cotangent,
    segment_ids,
    block_order,
    gain_attn,
    w_qkv,
    bias_q,
    bias_v,
    w_out,
    bias_out,
    gain_mlp,
    w_up,
    bias_up,
    w_down,
    bias_down,
):
    weights = (
        gain_attn,
        w_qkv,
        bias_q,
        bias_v,
        w_out,
        bias_out,
        gain_mlp,
        w_up,
        bias_up,
        w_down,
        bias_down,
    )
    batch_count = block_input.shape[0]
    row_count = block_input.shape[2]
    block_len = row_count // 2
    key_count = block_len * block_order.shape[0]
    layer_count = gain_attn.shape[0]
    head_dim = HD
    ctx_index = lax.axis_index("ctx")
    offsets = jnp.arange(block_len, dtype=jnp.int32)
    own_blocks = lax.dynamic_slice_in_dim(block_order, 2 * ctx_index, 2, 0)
    query_pos = (own_blocks[:, None] * block_len + offsets[None, :]).reshape(row_count)
    key_pos = (block_order[:, None] * block_len + offsets[None, :]).reshape(key_count)
    grad_totals = [None] * layer_count
    out_rows = []
    input_grads = []
    for micro_index in range(batch_count):
        query_seg = jnp.take(segment_ids[micro_index], query_pos, axis=1)
        key_seg = jnp.take(segment_ids[micro_index], key_pos, axis=1)
        allowed = (key_pos[None, None, :] <= query_pos[None, :, None]) & (
            key_seg[:, None, :] == query_seg[:, :, None]
        )
        hidden = block_input[micro_index].astype(jnp.float32)
        kept_layers = []
        for layer_index in range(layer_count):
            layer_weights = fetch_layer(weights, layer_index)
            hidden, kept_values = layer_forward(hidden, layer_weights, allowed, head_dim)
            kept_layers.append(kept_values)
        out_rows.append(hidden.astype(jnp.bfloat16))
        grad_carry = cotangent[micro_index].astype(jnp.float32)
        for layer_index in reversed(range(layer_count)):
            layer_weights = fetch_again(weights, layer_index)
            grad_carry, layer_grads = layer_backward(
                grad_carry, kept_layers[layer_index], layer_weights, allowed, head_dim
            )
            layer_grads = scatter_gradients(layer_grads)
            if grad_totals[layer_index] is None:
                grad_totals[layer_index] = layer_grads
            else:
                grad_totals[layer_index] = jax.tree.map(
                    jnp.add, grad_totals[layer_index], layer_grads
                )
        input_grads.append(grad_carry)
    grad_totals = [total_gradients(layer_grads) for layer_grads in grad_totals]
    stacked = [
        jnp.stack([grad_totals[layer_index][member] for layer_index in range(layer_count)])
        for member in range(11)
    ]
    return (
        jnp.stack(out_rows),
        jnp.stack(input_grads),
        stacked[0],
        stacked[1],
        stacked[2],
        stacked[3],
        stacked[4],
        stacked[5],
        stacked[6],
        stacked[7],
        stacked[8],
        stacked[9],
        stacked[10],
    )


def solution(mesh):
    in_specs = (
        P(None, "fsdp", "ctx", None),
        P(None, "fsdp", "ctx", None),
        P(None, "fsdp", None),
        P(),
        P(None, "fsdp"),
        P(None, "fsdp", None),
        P(None, "fsdp"),
        P(None, "fsdp"),
        P(None, "fsdp", None),
        P(None, "fsdp"),
        P(None, "fsdp"),
        P(None, "fsdp", None),
        P(None, "fsdp"),
        P(None, "fsdp", None),
        P(None, "fsdp"),
    )
    out_specs = (
        P(None, "fsdp", "ctx", None),
        P(None, "fsdp", "ctx", None),
        P(None, "fsdp"),
        P(None, "fsdp", None),
        P(None, "fsdp"),
        P(None, "fsdp"),
        P(None, "fsdp", None),
        P(None, "fsdp"),
        P(None, "fsdp"),
        P(None, "fsdp", None),
        P(None, "fsdp"),
        P(None, "fsdp", None),
        P(None, "fsdp"),
    )
    return jax.shard_map(shards, mesh=mesh, in_specs=in_specs, out_specs=out_specs, check_vma=False)
```

profile of v0, /device:TPU:0, one launch (start us, length us, event | category | flops | bytes accessed | tf_op | source)
XLA Modules:
  0.0 2571.8 jit_solution(6443045382317767936)
XLA Ops:
  14.7 18.8 all-reduce.51
  41.1 19.7 all-gather.55.cloned.1.call-done
  83.3 11.8 gather_fusion.1
  95.1 11.8 gather_fusion.3
  108.2 8.3 all-gather.8
  126.1 19.1 all-gather.41.cloned.1.call-done
  150.1 45.3 %while.128 = (s32[]{:T(128)}, bf16[6,1,256,128]{2,3,1,0:T(8,128)(2,1)S(1)}, f32[6,1,2,256]{3,2,1,0:T(2,128)S(1)}, s32[6]{0:T(128)S(1)}, bf16[1,2048,768]{1,2,0:T...) while((s32[]{:T(128)}, ...), condition=%wide.region_5.8_spmd.clone, body=%wide.region_2.0_spmd.clone.sunk | while | flops 282623488 | bytes 18254048 | solution.py:149
  198.9 15.0 all-gather.47.cloned.1.call-done
  218.7 33.9 %all-gather.49.cloned.1.call-done = bf16[1,2048,768]{2,1,0:T(8,128)(2,1)} async-done(((bf16[1,256,768]{2,1,0:T(8,128)(2,1)}), bf16[1,2048,768]{2,1,0:T(8,128)(2,1)}) %all-gather.49.cloned.1.call-update) | async-done | bytes 3145744 | tf_op jit(solution)/shard_map/all_gather | solution.py:220
  257.4 45.6 %while.130 = (s32[]{:T(128)}, bf16[6,1,256,128]{2,3,1,0:T(8,128)(2,1)S(1)}, f32[6,1,2,256]{3,2,1,0:T(2,128)S(1)}, s32[6]{0:T(128)S(1)}, bf16[1,2048,768]{1,2,0:T...) while((s32[]{:T(128)}, ...), condition=%wide.region_25.28_spmd.clone, body=%wide.region_22.27_spmd.clone.sunk | while | flops 282623488 | bytes 18254048 | solution.py:149
  316.5 54.0 %all-gather.61.cloned.1.call-done = bf16[1,3072,768]{2,1,0:T(8,128)(2,1)} async-done(((bf16[1,768,768]{2,1,0:T(8,128)(2,1)}), bf16[1,3072,768]{2,1,0:T(8,128)(2,1)}) %all-gather.61.cloned.1.call-update) | async-done | bytes 4718608 | tf_op jit(solution)/shard_map/all_gather | solution.py:40
  384.2 36.0 %all-gather.63.cloned.1.call-done = bf16[1,768,2304]{2,1,0:T(8,128)(2,1)} async-done(((bf16[1,192,2304]{2,1,0:T(8,128)(2,1)}), bf16[1,768,2304]{2,1,0:T(8,128)(2,1)}) %all-gather.63.cloned.1.call-update) | async-done | bytes 3538960 | tf_op jit(solution)/shard_map/all_gather | solution.py:32
  433.4 8.1 all-gather.19
  454.1 11.3 all-gather.43.cloned.1.call-done
  470.1 34.1 %all-gather.45.cloned.1.call-done = bf16[1,2048,768]{2,1,0:T(8,128)(2,1)} async-done(((bf16[1,256,768]{2,1,0:T(8,128)(2,1)}), bf16[1,2048,768]{2,1,0:T(8,128)(2,1)}) %all-gather.45.cloned.1.call-update) | async-done | bytes 3145744 | tf_op jit(solution)/shard_map/all_gather | solution.py:220
  509.0 40.3 %while.129 = (s32[]{:T(128)}, bf16[6,1,256,128]{2,3,1,0:T(8,128)(2,1)S(1)}, f32[6,1,2,256]{3,2,1,0:T(2,128)S(1)}, s32[6]{0:T(128)S(1)}, bf16[1,2048,768]{1,2,0:T...) while((s32[]{:T(128)}, ...), condition=%wide.region_15.18_spmd.clone, body=%wide.region_12.17_spmd.clone.sunk | while | flops 282623488 | bytes 18254048 | solution.py:149
  554.4 27.9 %all-gather.53.cloned.1.call-done = bf16[1,2048,768]{2,1,0:T(8,128)(2,1)} async-done(((bf16[1,256,768]{2,1,0:T(8,128)(2,1)}), bf16[1,2048,768]{2,1,0:T(8,128)(2,1)}) %all-gather.53.cloned.1.call-update) | async-done | bytes 3145744 | tf_op jit(solution)/shard_map/all_gather | solution.py:220
  587.1 45.6 %while.131 = (s32[]{:T(128)}, bf16[6,1,256,128]{2,3,1,0:T(8,128)(2,1)S(1)}, f32[6,1,2,256]{3,2,1,0:T(2,128)S(1)}, s32[6]{0:T(128)S(1)}, bf16[1,2048,768]{1,2,0:T...) while((s32[]{:T(128)}, ...), condition=%wide.region_35.38_spmd.clone, body=%wide.region_32.37_spmd.clone.sunk | while | flops 282623488 | bytes 18254048 | solution.py:149
  640.1 29.3 %all-gather.67.cloned.1.call-done = bf16[1,768,3072]{2,1,0:T(8,128)(2,1)} async-done(((bf16[1,192,3072]{2,1,0:T(8,128)(2,1)}), bf16[1,768,3072]{2,1,0:T(8,128)(2,1)}) %all-gather.67.cloned.1.call-update) | async-done | bytes 4718608 | tf_op jit(solution)/shard_map/all_gather | solution.py:38
  675.1 53.7 %all-gather.69.cloned.1.call-done = bf16[1,3072,768]{2,1,0:T(8,128)(2,1)} async-done(((bf16[1,768,768]{2,1,0:T(8,128)(2,1)}), bf16[1,3072,768]{2,1,0:T(8,128)(2,1)}) %all-gather.69.cloned.1.call-update) | async-done | bytes 4718608 | tf_op jit(solution)/shard_map/all_gather | solution.py:40
  728.8 7.5 fusion.356
  754.0 177.2 %while.134 = (s32[]{:T(128)}, bf16[6,1,256,128]{2,3,1,0:T(8,128)(2,1)S(1)}, bf16[6,1,2048,128]{2,3,1,0:T(8,128)(2,1)}, bf16[6,1,2048,128]{2,3,1,0:T(8,128)(2,1)}...) while((s32[]{:T(128)}, ...), condition=%wide.region_63.66_spmd.clone, body=%wide.region_61.65_spmd.clone.sunk | while | flops 687379456 | bytes 38101252 | solution.py:193
  941.9 181.3 %while.132 = (s32[]{:T(128)}, bf16[6,1,256,128]{2,3,1,0:T(8,128)(2,1)}, bf16[6,1,2048,128]{2,3,1,0:T(8,128)(2,1)}, bf16[6,1,2048,128]{2,3,1,0:T(8,128)(2,1)}, s3...) while((s32[]{:T(128)}, ...), condition=%wide.region_45.48_spmd.clone, body=%wide.region_43.47_spmd.clone.sunk | while | flops 687379456 | bytes 38101252 | solution.py:193
  953.7 7.2 fusion.537
  984.1 7.2 fusion.537
  1127.6 36.2 %reduce-scatter.27.cloned.1.call-done = bf16[1,256,768]{1,2,0:T(8,128)(2,1)} async-done(((bf16[1,2048,768]{1,2,0:T(8,128)(2,1)}), bf16[1,256,768]{1,2,0:T(8,128)(2,1)}) %reduce-scatter.27.cloned.1.call-update) | async-done | bytes 393232 | tf_op jit(solution)/shard_map/reduce_scatter | solution.py:322
  1163.8 41.7 %reduce-scatter.25.cloned.1.call-done = bf16[1,256,768]{1,2,0:T(8,128)(2,1)} async-done(((bf16[1,2048,768]{1,2,0:T(8,128)(2,1)}), bf16[1,256,768]{1,2,0:T(8,128)(2,1)}) %reduce-scatter.25.cloned.1.call-update) | async-done | bytes 393232 | tf_op jit(solution)/shard_map/reduce_scatter | solution.py:319
  1235.2 184.7 %while.135 = (s32[]{:T(128)}, bf16[6,1,256,128]{2,3,1,0:T(8,128)(2,1)}, bf16[6,1,2048,128]{2,3,1,0:T(8,128)(2,1)}, bf16[6,1,2048,128]{2,3,1,0:T(8,128)(2,1)}, s3...) while((s32[]{:T(128)}, ...), condition=%wide.region_72.75_spmd.clone, body=%wide.region_70.74_spmd.clone.sunk | while | flops 687379456 | bytes 38363420 | solution.py:193
  1441.9 186.6 %while.133 = (s32[]{:T(128)}, bf16[6,1,256,128]{2,3,1,0:T(8,128)(2,1)}, bf16[6,1,2048,128]{2,3,1,0:T(8,128)(2,1)}, bf16[6,1,2048,128]{2,3,1,0:T(8,128)(2,1)}, s3...) while((s32[]{:T(128)}, ...), condition=%wide.region_54.57_spmd.clone, body=%wide.region_52.56_spmd.clone.sunk | while | flops 687379456 | bytes 38363420 | solution.py:193
  1465.1 7.2 fusion.553
  1485.9 7.2 fusion.551
  1548.1 7.2 fusion.551
  1579.0 7.2 fusion.551
  1610.0 7.3 fusion.551
  1716.0 54.8 %reduce-scatter.71.cloned.1.call-done = bf16[768,768]{1,0:T(8,128)(2,1)} async-done(((bf16[3072,768]{1,0:T(8,128)(2,1)}), bf16[768,768]{1,0:T(8,128)(2,1)}) %reduce-scatter.71.cloned.1.call-update) | async-done | bytes 1179664 | tf_op jit(solution)/shard_map/reduce_scatter | solution.py:90
  1770.8 60.0 %reduce-scatter.69.cloned.1.call-done = bf16[768,768]{1,0:T(8,128)(2,1)} async-done(((bf16[3072,768]{1,0:T(8,128)(2,1)}), bf16[768,768]{1,0:T(8,128)(2,1)}) %reduce-scatter.69.cloned.1.call-update) | async-done | bytes 1179664 | tf_op jit(solution)/shard_map/reduce_scatter | solution.py:90
  1833.7 57.7 %reduce-scatter.63.cloned.1.call-done = bf16[192,3072]{1,0:T(8,128)(2,1)} async-done(((bf16[768,3072]{1,0:T(8,128)(2,1)}), bf16[192,3072]{1,0:T(8,128)(2,1)}) %reduce-scatter.63.cloned.1.call-update) | async-done | bytes 1179664 | tf_op jit(solution)/shard_map/reduce_scatter | solution.py:84
  1891.4 60.7 %reduce-scatter.61.cloned.1.call-done = bf16[192,3072]{1,0:T(8,128)(2,1)} async-done(((bf16[768,3072]{1,0:T(8,128)(2,1)}), bf16[192,3072]{1,0:T(8,128)(2,1)}) %reduce-scatter.61.cloned.1.call-update) | async-done | bytes 1179664 | tf_op jit(solution)/shard_map/reduce_scatter | solution.py:84
  1965.5 20.4 all-reduce.50
  2005.5 50.3 %reduce-scatter.45.cloned.1.call-done = bf16[192,2304]{1,0:T(8,128)(2,1)} async-done(((bf16[768,2304]{1,0:T(8,128)(2,1)}), bf16[192,2304]{1,0:T(8,128)(2,1)}) %reduce-scatter.45.cloned.1.call-update) | async-done | bytes 884752 | tf_op jit(solution)/shard_map/reduce_scatter | solution.py:66
  2058.3 57.6 %reduce-scatter.67.cloned.1.call-done = bf16[768,768]{1,0:T(8,128)(2,1)} async-done(((bf16[3072,768]{1,0:T(8,128)(2,1)}), bf16[768,768]{1,0:T(8,128)(2,1)}) %reduce-scatter.67.cloned.1.call-update) | async-done | bytes 1179664 | tf_op jit(solution)/shard_map/reduce_scatter | solution.py:90
  2115.9 60.0 %reduce-scatter.65.cloned.1.call-done = bf16[768,768]{1,0:T(8,128)(2,1)} async-done(((bf16[3072,768]{1,0:T(8,128)(2,1)}), bf16[768,768]{1,0:T(8,128)(2,1)}) %reduce-scatter.65.cloned.1.call-update) | async-done | bytes 1179664 | tf_op jit(solution)/shard_map/reduce_scatter | solution.py:90
  2178.8 57.1 %reduce-scatter.59.cloned.1.call-done = bf16[192,3072]{1,0:T(8,128)(2,1)} async-done(((bf16[768,3072]{1,0:T(8,128)(2,1)}), bf16[192,3072]{1,0:T(8,128)(2,1)}) %reduce-scatter.59.cloned.1.call-update) | async-done | bytes 1179664 | tf_op jit(solution)/shard_map/reduce_scatter | solution.py:84
  2235.9 60.1 %reduce-scatter.57.cloned.1.call-done = bf16[192,3072]{1,0:T(8,128)(2,1)} async-done(((bf16[768,3072]{1,0:T(8,128)(2,1)}), bf16[192,3072]{1,0:T(8,128)(2,1)}) %reduce-scatter.57.cloned.1.call-update) | async-done | bytes 1179664 | tf_op jit(solution)/shard_map/reduce_scatter | solution.py:84
  2299.0 47.1 %reduce-scatter.43.cloned.1.call-done = bf16[192,2304]{1,0:T(8,128)(2,1)} async-done(((bf16[768,2304]{1,0:T(8,128)(2,1)}), bf16[192,2304]{1,0:T(8,128)(2,1)}) %reduce-scatter.43.cloned.1.call-update) | async-done | bytes 884752 | tf_op jit(solution)/shard_map/reduce_scatter | solution.py:66
  2346.2 50.3 %reduce-scatter.41.cloned.1.call-done = bf16[192,2304]{1,0:T(8,128)(2,1)} async-done(((bf16[768,2304]{1,0:T(8,128)(2,1)}), bf16[192,2304]{1,0:T(8,128)(2,1)}) %reduce-scatter.41.cloned.1.call-update) | async-done | bytes 884752 | tf_op jit(solution)/shard_map/reduce_scatter | solution.py:66
  2407.8 30.2 %all-reduce.48 = (bf16[1,192]{1,0:T(2,128)(2,1)S(1)}, bf16[1,192]{1,0:T(2,128)(2,1)S(1)}, bf16[1,192]{1,0:T(2,128)(2,1)S(1)}, bf16[1,192]{1,0:T(2,128)(2,1)S(1)}...) all-reduce(bf16[1,192]{1,0:T(2,128)(2,1)S(1)} %stack.179, ...), channel_id=1, replica_groups=mesh['ctx'=8,'fsdp'=4] {'ctx'}, use_global_device_ids=true, to_apply=%region_85.88 | all-reduce | flops 3840 | bytes 15360 | tf_op jit(solution)/shard_map/psum | solution.py:101
  2442.1 112.7 %all-reduce.54.cloned.1.call-done = (bf16[1,192,2304]{2,1,0:T(8,128)(2,1)}, bf16[1,192,2304]{2,1,0:T(8,128)(2,1)}, bf16[1,192,768]{2,1,0:T(8,128)(2,1)}, bf16[1,...) async-done(((bf16[1,192,2304]{2,1,0:T(8,128)(2,1)}, ...) | async-done | bytes 7077904 | tf_op jit(solution)/shard_map/psum | solution.py:102
  (1439 shorter events, 1209.1 us)
Async XLA Ops:
  7.3 53.5 %all-gather.55.cloned.1.call-start = ((), (), s32[]{:S(2)}) async-start(), calls=%async_computation.56 | async-start | bytes 4423680 | tf_op jit(solution)/shard_map/all_gather | solution.py:32
  10.2 111.3 %all-gather.39.cloned.1.call-start = ((), (), s32[]{:S(2)}) async-start(), calls=%async_computation.24 | async-start | bytes 3538944 | tf_op jit(solution)/shard_map/all_gather | solution.py:221
  68.0 77.3 %all-gather.41.cloned.1.call-start = ((), (), s32[]{:S(2)}) async-start(), calls=%async_computation.25 | async-start | bytes 3538944 | tf_op jit(solution)/shard_map/all_gather | solution.py:220
  69.9 125.5 %all-gather.57.cloned.1.call-start = ((), (), s32[]{:S(2)}) async-start(), calls=%async_computation.57 | async-start | bytes 1474560 | tf_op jit(solution)/shard_map/all_gather | solution.py:35
  71.9 142.0 %all-gather.47.cloned.1.call-start = ((), (), s32[]{:S(2)}) async-start(), calls=%async_computation.28 | async-start | bytes 3538944 | tf_op jit(solution)/shard_map/all_gather | solution.py:221
  72.5 180.1 %all-gather.49.cloned.1.call-start = ((), (), s32[]{:S(2)}) async-start(), calls=%async_computation.29 | async-start | bytes 3538944 | tf_op jit(solution)/shard_map/all_gather | solution.py:220
  73.4 237.6 %all-gather.59.cloned.1.call-start = ((), (), s32[]{:S(2)}) async-start(), calls=%async_computation.58 | async-start | bytes 5898240 | tf_op jit(solution)/shard_map/all_gather | solution.py:38
  76.9 293.6 %all-gather.61.cloned.1.call-start = ((), (), s32[]{:S(2)}) async-start(), calls=%async_computation.59 | async-start | bytes 5898240 | tf_op jit(solution)/shard_map/all_gather | solution.py:40
  78.6 341.7 %all-gather.63.cloned.1.call-start = ((), (), s32[]{:S(2)}) async-start(), calls=%async_computation.60 | async-start | bytes 4423680 | tf_op jit(solution)/shard_map/all_gather | solution.py:32
  79.3 386.1 %all-gather.43.cloned.1.call-start = ((), (), s32[]{:S(2)}) async-start(), calls=%async_computation.26 | async-start | bytes 3538944 | tf_op jit(solution)/shard_map/all_gather | solution.py:221
  197.8 185.5 %copy-start = (f32[1,256,767]{2,1,0:T(8,128)}, f32[1,256,767]{2,1,0:T(8,128)S(1)}, u32[]{:S(2)}) copy-start(f32[1,256,767]{2,1,0:T(8,128)S(1)} %get-tuple-element.1897) | copy-start | bytes 2356228
  198.9 178.1 %copy-start.71 = (f32[256,1]{1,0:T(8,128)}, f32[256,1]{1,0:T(8,128)S(1)}, u32[]{:S(2)}) copy-start(f32[256,1]{1,0:T(8,128)S(1)} %copy.118) | copy-start | bytes 3076
  383.5 826.3 %copy-start.4 = (f32[1,256,767]{2,1,0:T(8,128)}, f32[1,256,767]{2,1,0:T(8,128)S(1)}, u32[]{:S(2)}) copy-start(f32[1,256,767]{2,1,0:T(8,128)S(1)} %get-tuple-element.1895) | copy-start | bytes 2356228
  426.9 77.3 %all-gather.45.cloned.1.call-start = ((), (), s32[]{:S(2)}) async-start(), calls=%async_computation.27 | async-start | bytes 3538944 | tf_op jit(solution)/shard_map/all_gather | solution.py:220
  429.0 120.3 %all-gather.51.cloned.1.call-start = ((), (), s32[]{:S(2)}) async-start(), calls=%async_computation.30 | async-start | bytes 3538944 | tf_op jit(solution)/shard_map/all_gather | solution.py:221
  429.6 152.7 %all-gather.53.cloned.1.call-start = ((), (), s32[]{:S(2)}) async-start(), calls=%async_computation.31 | async-start | bytes 3538944 | tf_op jit(solution)/shard_map/all_gather | solution.py:220
  431.6 201.1 %all-gather.65.cloned.1.call-start = ((), (), s32[]{:S(2)}) async-start(), calls=%async_computation.61 | async-start | bytes 1474560 | tf_op jit(solution)/shard_map/all_gather | solution.py:35
  432.2 237.2 %all-gather.67.cloned.1.call-start = ((), (), s32[]{:S(2)}) async-start(), calls=%async_computation.62 | async-start | bytes 5898240 | tf_op jit(solution)/shard_map/all_gather | solution.py:38
  432.7 296.0 %all-gather.69.cloned.1.call-start = ((), (), s32[]{:S(2)}) async-start(), calls=%async_computation.63 | async-start | bytes 5898240 | tf_op jit(solution)/shard_map/all_gather | solution.py:40
  433.3 690.7 %reduce-scatter.35.cloned.1.call-start = ((), (), s32[]{:S(2)}) async-start(), calls=%async_computation.37 | async-start | bytes 3538944 | tf_op jit(solution)/shard_map/reduce_scatter | solution.py:322
  433.4 312.0 %copy-start.109 = (f32[768]{0:T(1024)}, f32[768]{0:T(1024)S(1)}, u32[]{:S(2)}) copy-start(f32[768]{0:T(1024)S(1)} %convert_element_type.1194) | copy-start | bytes 9220
  637.9 107.5 %copy-start.6 = (f32[1,256,767]{2,1,0:T(8,128)}, f32[1,256,767]{2,1,0:T(8,128)S(1)}, u32[]{:S(2)}) copy-start(f32[1,256,767]{2,1,0:T(8,128)S(1)} %get-tuple-element.1893) | copy-start | bytes 2356228
  931.2 192.9 %copy-start.65 = (bf16[6,1,256,128]{2,3,1,0:T(8,128)(2,1)}, bf16[6,1,256,128]{2,3,1,0:T(8,128)(2,1)S(1)}, u32[]{:S(2)}) copy-start(bf16[6,1,256,128]{2,3,1,0:T(8,128)(2,1)S(1)} %get-tuple-element.992) | copy-start | bytes 1179652
  931.2 192.9 %reduce-scatter.33.cloned.1.call-start = ((), (), s32[]{:S(2)}) async-start(), calls=%async_computation.36 | async-start | bytes 3538944 | tf_op jit(solution)/shard_map/reduce_scatter | solution.py:319
  934.4 229.4 %reduce-scatter.27.cloned.1.call-start = ((), (), s32[]{:S(2)}) async-start(), calls=%async_computation.33 | async-start | bytes 3538944 | tf_op jit(solution)/shard_map/reduce_scatter | solution.py:322
  1123.2 82.2 %reduce-scatter.25.cloned.1.call-start = ((), (), s32[]{:S(2)}) async-start(), calls=%async_computation.32 | async-start | bytes 3538944 | tf_op jit(solution)/shard_map/reduce_scatter | solution.py:319
  1123.8 568.8 %reduce-scatter.39.cloned.1.call-start = ((), (), s32[]{:S(2)}) async-start(), calls=%async_computation.39 | async-start | bytes 3538944 | tf_op jit(solution)/shard_map/reduce_scatter | solution.py:322
  1419.9 272.8 %reduce-scatter.37.cloned.1.call-start = ((), (), s32[]{:S(2)}) async-start(), calls=%async_computation.38 | async-start | bytes 3538944 | tf_op jit(solution)/shard_map/reduce_scatter | solution.py:319
  1420.7 280.4 %reduce-scatter.55.cloned.1.call-start = ((), (), s32[]{:S(2)}) async-start(), calls=%async_computation.47 | async-start | bytes 1474560 | tf_op jit(solution)/shard_map/reduce_scatter | solution.py:75
  1423.4 277.7 %reduce-scatter.53.cloned.1.call-start = ((), (), s32[]{:S(2)}) async-start(), calls=%async_computation.46 | async-start | bytes 1474560 | tf_op jit(solution)/shard_map/reduce_scatter | solution.py:75
  1426.0 281.0 %reduce-scatter.51.cloned.1.call-start = ((), (), s32[]{:S(2)}) async-start(), calls=%async_computation.45 | async-start | bytes 1474560 | tf_op jit(solution)/shard_map/reduce_scatter | solution.py:75
  1428.7 278.3 %reduce-scatter.49.cloned.1.call-start = ((), (), s32[]{:S(2)}) async-start(), calls=%async_computation.44 | async-start | bytes 1474560 | tf_op jit(solution)/shard_map/reduce_scatter | solution.py:75
  1434.5 274.3 %reduce-scatter.31.cloned.1.call-start = ((), (), s32[]{:S(2)}) async-start(), calls=%async_computation.35 | async-start | bytes 3538944 | tf_op jit(solution)/shard_map/reduce_scatter | solution.py:322
  1628.6 82.9 %reduce-scatter.29.cloned.1.call-start = ((), (), s32[]{:S(2)}) async-start(), calls=%async_computation.34 | async-start | bytes 3538944 | tf_op jit(solution)/shard_map/reduce_scatter | solution.py:319
  1629.3 141.4 %reduce-scatter.71.cloned.1.call-start = ((), (), s32[]{:S(2)}) async-start(), calls=%async_computation.55 | async-start | bytes 5898240 | tf_op jit(solution)/shard_map/reduce_scatter | solution.py:90
  1635.9 194.8 %reduce-scatter.69.cloned.1.call-start = ((), (), s32[]{:S(2)}) async-start(), calls=%async_computation.54 | async-start | bytes 5898240 | tf_op jit(solution)/shard_map/reduce_scatter | solution.py:90
  1643.2 248.3 %reduce-scatter.63.cloned.1.call-start = ((), (), s32[]{:S(2)}) async-start(), calls=%async_computation.51 | async-start | bytes 5898240 | tf_op jit(solution)/shard_map/reduce_scatter | solution.py:84
  1649.5 302.7 %reduce-scatter.61.cloned.1.call-start = ((), (), s32[]{:S(2)}) async-start(), calls=%async_computation.50 | async-start | bytes 5898240 | tf_op jit(solution)/shard_map/reduce_scatter | solution.py:84
  1655.8 349.7 %reduce-scatter.47.cloned.1.call-start = ((), (), s32[]{:S(2)}) async-start(), calls=%async_computation.43 | async-start | bytes 4423680 | tf_op jit(solution)/shard_map/reduce_scatter | solution.py:66
  1661.0 394.8 %reduce-scatter.45.cloned.1.call-start = ((), (), s32[]{:S(2)}) async-start(), calls=%async_computation.42 | async-start | bytes 4423680 | tf_op jit(solution)/shard_map/reduce_scatter | solution.py:66
  1666.5 449.5 %reduce-scatter.67.cloned.1.call-start = ((), (), s32[]{:S(2)}) async-start(), calls=%async_computation.53 | async-start | bytes 5898240 | tf_op jit(solution)/shard_map/reduce_scatter | solution.py:90
  1673.8 502.1 %reduce-scatter.65.cloned.1.call-start = ((), (), s32[]{:S(2)}) async-start(), calls=%async_computation.52 | async-start | bytes 5898240 | tf_op jit(solution)/shard_map/reduce_scatter | solution.py:90
  1681.2 554.7 %reduce-scatter.59.cloned.1.call-start = ((), (), s32[]{:S(2)}) async-start(), calls=%async_computation.49 | async-start | bytes 5898240 | tf_op jit(solution)/shard_map/reduce_scatter | solution.py:84
  1687.2 608.8 %reduce-scatter.57.cloned.1.call-start = ((), (), s32[]{:S(2)}) async-start(), calls=%async_computation.48 | async-start | bytes 5898240 | tf_op jit(solution)/shard_map/reduce_scatter | solution.py:84
  1692.4 653.8 %reduce-scatter.43.cloned.1.call-start = ((), (), s32[]{:S(2)}) async-start(), calls=%async_computation.41 | async-start | bytes 4423680 | tf_op jit(solution)/shard_map/reduce_scatter | solution.py:66
  1697.8 698.7 %reduce-scatter.41.cloned.1.call-start = ((), (), s32[]{:S(2)}) async-start(), calls=%async_computation.40 | async-start | bytes 4423680 | tf_op jit(solution)/shard_map/reduce_scatter | solution.py:66
  1716.0 242.8 %copy-start.14 = (bf16[1,768,2304]{2,1,0:T(8,128)(2,1)S(1)}, bf16[1,768,2304]{2,1,0:T(8,128)(2,1)}, u32[]{:S(2)}) copy-start(bf16[1,768,2304]{2,1,0:T(8,128)(2,1)} %all-gather.55.cloned.1.call-done) | copy-start | bytes 10616836
  1716.0 838.8 %all-reduce.54.cloned.1.call-start = ((), (), s32[]{:S(2)}) async-start(), calls=%async_computation.64 | async-start | bytes 14155776 | tf_op jit(solution)/shard_map/psum | solution.py:102
  (207 other events, 2551.0 us)
Sparse Core Ops, SparseCore 0:
  10.5 50.2 all-gather.54
  68.1 38.2 all-gather.38
  108.0 37.1 all-gather.40
  146.9 26.5 all-gather.56
  175.6 38.2 all-gather.46
  215.4 37.1 all-gather.48
  255.0 55.9 all-gather.58
  313.5 57.0 all-gather.60
  372.9 47.2 all-gather.62
  427.1 38.2 all-gather.42
  467.0 37.1 all-gather.44
  505.7 37.1 all-gather.50
  545.1 37.1 all-gather.52
  584.0 26.5 all-gather.64
  612.3 57.0 all-gather.66
  671.6 57.0 all-gather.68
  931.3 40.3 reduce-scatter.34
  973.9 39.3 reduce-scatter.32
  1123.4 40.3 reduce-scatter.26
  1165.9 39.4 reduce-scatter.24
  1420.0 39.4 reduce-scatter.38
  1461.8 39.4 reduce-scatter.36
  1504.8 27.6 reduce-scatter.54
  1535.8 28.5 reduce-scatter.52
  1567.3 28.5 reduce-scatter.50
  1598.6 28.5 reduce-scatter.48
  1629.4 40.3 reduce-scatter.30
  1672.1 39.4 reduce-scatter.28
  1714.5 56.1 reduce-scatter.70
  1773.6 57.0 reduce-scatter.68
  1834.3 57.0 reduce-scatter.62
  1895.0 57.0 reduce-scatter.60
  1955.7 49.7 reduce-scatter.46
  2008.5 47.2 reduce-scatter.44
  2058.8 57.0 reduce-scatter.66
  2118.8 57.0 reduce-scatter.64
  2178.7 57.0 reduce-scatter.58
  2238.9 57.0 reduce-scatter.56
  2298.9 47.2 reduce-scatter.42
  2349.3 47.2 reduce-scatter.40
  2400.7 154.0 all-reduce.53
where the time goes:
time: 2590 us; the launch traced here: 2570 us
  waiting for transfers between devices  1160 us (45%)
  matrix products  771 us (30%)
  local copies, waits for them, and re-layouts  366 us (14%)
  other arithmetic  130 us (5%)
  blocking collectives  85.8 us (3%)
  loops' own time  35.4 us (1%)
    reduce_scatter x4, waiting for transfers between devices, scatter_gradients(): lax.psum_scatter(grads[7].astype(jnp.bfloat16), 'fsdp', scatter_dimension...  236 us
    reduce_scatter x4, waiting for transfers between devices, scatter_gradients(): lax.psum_scatter(grads[9].astype(jnp.bfloat16), 'fsdp', scatter_dimension...  232 us
    dot_general x24, matrix products, one_pair(): jnp.einsum('sgqk,skgd->sqgd', grad_raw, key_pair, preferred_element_type=...  170 us
    dot_general x24, matrix products, one_pair(): jnp.einsum('sgqk,sqgd->skgd', grad_raw, query_pair, preferred_element_typ...  168 us
    reduce_scatter x4, waiting for transfers between devices, scatter_gradients(): lax.psum_scatter(grads[1].astype(jnp.bfloat16), 'fsdp', scatter_dimension...  153 us
    dynamic_slice x168, local copies, waits for them, and re-layouts, pair_slice(): lax.dynamic_slice_in_dim(matrix, pair_index * 2 * head_dim, 2 * head_dim, 2)  142 us
    all_gather x4, waiting for transfers between devices, layer_forward(): lax.all_gather(key_rows, 'ctx', axis=1, tiled=True)  115 us
    psum x1, waiting for transfers between devices, total_gradients(): lax.psum(grads[1].astype(jnp.bfloat16), 'ctx').astype(jnp.float32)  113 us
  transfers between devices with their start and end apart: 41, of which 28 were waited for; matrix products, arithmetic and copies ran while one was open for 32% of the time, Pallas kernels for 0%

commit v1 on v0

v1 whole, which is shorter than its diff:
```python
from functools import partial

import jax
import jax.numpy as jnp
from jax import lax
from jax.experimental import pallas as pl
from jax.experimental.pallas import tpu as pltpu
from jax.sharding import PartitionSpec as P

HD = 64
EPS = 1e-06
NEG = -1e30
BF = jnp.bfloat16
F32 = jnp.float32
QT = 256


def tile_spans(rows, halo, tile):
    return [(i, (i, halo), (0, i + tile)) for i in range(0, rows, tile)]


def tile_masks(seg_q, seg_own, seg_halo, row0, halo_span, own_span, tile):
    h0, h1 = halo_span
    o0, o1 = own_span
    seg_rows = seg_q[row0 : row0 + tile, :]
    row = row0 + lax.broadcasted_iota(jnp.int32, (tile, o1 - o0), 0)
    col = o0 + lax.broadcasted_iota(jnp.int32, (tile, o1 - o0), 1)
    own = (seg_rows == seg_own[:, o0:o1]) & (col <= row)
    past = seg_rows == seg_halo[:, h0:h1] if h1 > h0 else None
    return past, own


def dot_t(a, b):
    return lax.dot_general(a, b, (((1,), (1,)), ((), ())), preferred_element_type=F32)


def dot_n(a, b):
    return lax.dot_general(a, b, (((1,), (0,)), ((), ())), preferred_element_type=F32)


def dot_l(a, b):
    return lax.dot_general(a, b, (((0,), (0,)), ((), ())), preferred_element_type=F32)


def attend_kernel(q_ref, k_ref, v_ref, kh_ref, vh_ref, sq_ref, so_ref, sh_ref, o_ref, lse_ref):
    rows, halo = q_ref.shape[0], kh_ref.shape[0]
    scale = HD ** (-0.5)
    seg_q, seg_own, seg_halo = sq_ref[...], so_ref[...], sh_ref[...]
    for row0, (h0, h1), (o0, o1) in tile_spans(rows, halo, QT):
        past, own = tile_masks(seg_q, seg_own, seg_halo, row0, (h0, h1), (o0, o1), QT)
        for j in range(2):
            cols = slice(j * HD, (j + 1) * HD)
            q = q_ref[row0 : row0 + QT, cols]
            s_own = jnp.where(own, dot_t(q, k_ref[o0:o1, cols]) * scale, NEG)
            top = jnp.max(s_own, axis=-1, keepdims=True)
            if past is not None:
                s_past = jnp.where(past, dot_t(q, kh_ref[h0:h1, cols]) * scale, NEG)
                top = jnp.maximum(top, jnp.max(s_past, axis=-1, keepdims=True))
            e_own = jnp.exp(s_own - top)
            total = jnp.sum(e_own, axis=-1, keepdims=True)
            out = dot_n(e_own.astype(BF), v_ref[o0:o1, cols])
            if past is not None:
                e_past = jnp.exp(s_past - top)
                total = total + jnp.sum(e_past, axis=-1, keepdims=True)
                out = out + dot_n(e_past.astype(BF), vh_ref[h0:h1, cols])
            o_ref[row0 : row0 + QT, cols] = (out / total).astype(BF)
            lse_ref[row0 : row0 + QT, cols] = jnp.broadcast_to(top + jnp.log(total), (QT, HD))


def attend_forward(qkv, kv_halo, segs):
    rows, width = qkv.shape[0], qkv.shape[1] // 3
    halo = kv_halo.shape[0]
    pairs = width // (2 * HD)
    seg_q, seg_own, seg_halo = segs
    col = lambda off: (lambda h: (0, off + h))
    fixed = lambda h: (0, 0)
    return pl.pallas_call(
        attend_kernel,
        name="attend_forward",
        grid=(pairs,),
        in_specs=[
            pl.BlockSpec((rows, 2 * HD), col(0)),
            pl.BlockSpec((rows, 2 * HD), col(pairs)),
            pl.BlockSpec((rows, 2 * HD), col(2 * pairs)),
            pl.BlockSpec((halo, 2 * HD), col(0)),
            pl.BlockSpec((halo, 2 * HD), col(pairs)),
            pl.BlockSpec((rows, 1), fixed),
            pl.BlockSpec((1, rows), fixed),
            pl.BlockSpec((1, halo), fixed),
        ],
        out_specs=[
            pl.BlockSpec((rows, 2 * HD), col(0)),
            pl.BlockSpec((rows, 2 * HD), col(0)),
        ],
        out_shape=[
            jax.ShapeDtypeStruct((rows, width), BF),
            jax.ShapeDtypeStruct((rows, width), F32),
        ],
        cost_estimate=pl.CostEstimate(
            flops=4 * rows * (rows + halo) * width,
            transcendentals=rows * (rows + halo) * pairs * 2,
            bytes_accessed=12 * rows * width,
        ),
    )(qkv, qkv, qkv, kv_halo, kv_halo, seg_q, seg_own, seg_halo)


def attend_back_kernel(
    q_ref, k_ref, v_ref, kh_ref, vh_ref, do_ref, lse_ref, sq_ref, so_ref, sh_ref,
    dq_ref, dk_ref, dv_ref, dkh_ref, dvh_ref,
    ak_ref, av_ref, akh_ref, avh_ref,
):
    rows, halo = q_ref.shape[0], kh_ref.shape[0]
    scale = HD ** (-0.5)
    seg_q, seg_own, seg_halo = sq_ref[...], so_ref[...], sh_ref[...]
    for ref in (ak_ref, av_ref, akh_ref, avh_ref):
        ref[...] = jnp.zeros_like(ref)
    for row0, (h0, h1), (o0, o1) in tile_spans(rows, halo, QT):
        past, own = tile_masks(seg_q, seg_own, seg_halo, row0, (h0, h1), (o0, o1), QT)
        tile = slice(row0, row0 + QT)
        for j in range(2):
            cols = slice(j * HD, (j + 1) * HD)
            q = q_ref[tile, cols]
            do = do_ref[tile, cols]
            lse = lse_ref[tile, j * HD : j * HD + 1]
            parts = [(own, k_ref, v_ref, ak_ref, av_ref, slice(o0, o1))]
            if past is not None:
                parts.append((past, kh_ref, vh_ref, akh_ref, avh_ref, slice(h0, h1)))
            work = []
            inner = jnp.zeros((QT, 1), F32)
            for mask, kr, vr, akr, avr, span in parts:
                k, v = kr[span, cols], vr[span, cols]
                p = jnp.exp(jnp.where(mask, dot_t(q, k) * scale, NEG) - lse)
                dp = dot_t(do, v)
                inner = inner + jnp.sum(p * dp, axis=-1, keepdims=True)
                work.append((p, dp, k, akr, avr, span))
            dq = jnp.zeros((QT, HD), F32)
            for p, dp, k, akr, avr, span in work:
                ds = (p * (dp - inner) * scale).astype(BF)
                dq = dq + dot_n(ds, k)
                akr[span, cols] += dot_l(ds, q)
                avr[span, cols] += dot_l(p.astype(BF), do)
            dq_ref[tile, cols] = dq.astype(BF)
    dk_ref[...] = ak_ref[...]
    dv_ref[...] = av_ref[...]
    dkh_ref[...] = akh_ref[...].astype(BF)
    dvh_ref[...] = avh_ref[...].astype(BF)


def attend_backward(qkv, kv_halo, segs, lse, d_mixed):
    rows, width = qkv.shape[0], qkv.shape[1] // 3
    halo = kv_halo.shape[0]
    pairs = width // (2 * HD)
    seg_q, seg_own, seg_halo = segs
    col = lambda off: (lambda h: (0, off + h))
    fixed = lambda h: (0, 0)
    own = lambda off: pl.BlockSpec((rows, 2 * HD), col(off))
    past = lambda off: pl.BlockSpec((halo, 2 * HD), col(off))
    return pl.pallas_call(
        attend_back_kernel,
        name="attend_backward",
        grid=(pairs,),
        in_specs=[
            own(0), own(pairs), own(2 * pairs), past(0), past(pairs), own(0), own(0),
            pl.BlockSpec((rows, 1), fixed),
            pl.BlockSpec((1, rows), fixed),
            pl.BlockSpec((1, halo), fixed),
        ],
        out_specs=[own(0), own(0), own(0), past(0), past(0)],
        out_shape=[
            jax.ShapeDtypeStruct((rows, width), BF),
            jax.ShapeDtypeStruct((rows, width), F32),
            jax.ShapeDtypeStruct((rows, width), F32),
            jax.ShapeDtypeStruct((halo, width), BF),
            jax.ShapeDtypeStruct((halo, width), BF),
        ],
        scratch_shapes=[
            pltpu.VMEM((rows, 2 * HD), F32),
            pltpu.VMEM((rows, 2 * HD), F32),
            pltpu.VMEM((halo, 2 * HD), F32),
            pltpu.VMEM((halo, 2 * HD), F32),
        ],
        cost_estimate=pl.CostEstimate(
            flops=10 * rows * (rows + halo) * width,
            transcendentals=rows * (rows + halo) * pairs * 2,
            bytes_accessed=30 * rows * width,
        ),
    )(qkv, qkv, qkv, kv_halo, kv_halo, d_mixed, lse, seg_q, seg_own, seg_halo)


def mm(a, w):
    return jnp.dot(a, w, preferred_element_type=F32)


def mm_t(a, w):
    return lax.dot_general(a, w, (((1,), (1,)), ((), ())), preferred_element_type=F32)


def mm_l(a, b):
    return lax.dot_general(a, b, (((0,), (0,)), ((), ())), preferred_element_type=F32)


def off_mean(y):
    return y - jnp.mean(y, axis=-1, keepdims=True)


def inverse_rms(u):
    return lax.rsqrt(jnp.mean(u * u, axis=-1, keepdims=True) + EPS)


def halo_of(x, halo_steps, runs, axis_size):
    parts = []
    for step in range(halo_steps, 0, -1):
        pairs = [(i, i + step) for i in range(axis_size - step) if i % runs + step < runs]
        parts.append(lax.ppermute(x, "ctx", pairs))
    return jnp.concatenate(parts, axis=0) if len(parts) > 1 else parts[0]


def halo_back(d, own, halo_steps, runs, axis_size):
    rows = own.shape[0]
    for n, step in enumerate(range(halo_steps, 0, -1)):
        pairs = [(i + step, i) for i in range(axis_size - step) if i % runs + step < runs]
        own = own + lax.ppermute(d[n * rows : (n + 1) * rows], "ctx", pairs).astype(F32)
    return own


def layer_forward(u, w, segs, shift):
    gain_attn, w_qkv, bias_q, bias_v, w_out, bias_out, gain_mlp, w_up, bias_up, w_down, bias_down = w
    width = w_out.shape[0]
    a1 = (u * inverse_rms(u) * gain_attn).astype(BF)
    bias = jnp.concatenate([bias_q, jnp.zeros_like(bias_q), bias_v])
    qkv = (mm(a1, w_qkv) + bias).astype(BF)
    kv_halo = halo_of(qkv[:, width:], *shift)
    mixed, lse = attend_forward(qkv, kv_halo, segs)
    u1 = u + off_mean(mm(mixed, w_out) + bias_out)
    a2 = (u1 * inverse_rms(u1) * gain_mlp).astype(BF)
    z = mm(a2, w_up) + bias_up
    act = jax.nn.gelu(z, approximate=True).astype(BF)
    u2 = u1 + off_mean(mm(act, w_down) + bias_down)
    return u2, (u, a1, qkv, kv_halo, mixed, lse, u1, a2, z, act)


def norm_backward(d_normed, u, gain):
    r = inverse_rms(u)
    n = u * r
    d_gain = jnp.sum(d_normed * n, axis=0)
    e = d_normed * gain
    return r * (e - n * jnp.mean(e * n, axis=-1, keepdims=True)), d_gain


def column_sums(x):
    return jnp.sum(x.astype(F32), axis=0)


def layer_backward(g, kept, w, segs, shift):
    gain_attn, w_qkv, bias_q, bias_v, w_out, bias_out, gain_mlp, w_up, bias_up, w_down, bias_down = w
    u, a1, qkv, kv_halo, mixed, lse, u1, a2, z, act = kept
    width = w_out.shape[0]
    dy2 = off_mean(g).astype(BF)
    dw_down = mm_l(act, dy2)
    d_act = mm_t(dy2, w_down)
    pull = jax.vjp(partial(jax.nn.gelu, approximate=True), z)[1]
    dz = pull(d_act)[0].astype(BF)
    dw_up = mm_l(a2, dz)
    du1, dgain_mlp = norm_backward(mm_t(dz, w_up), u1, gain_mlp)
    g = g + du1
    dy = off_mean(g).astype(BF)
    dw_out = mm_l(mixed, dy)
    d_mixed = mm_t(dy, w_out).astype(BF)
    dq, dk, dv, dkh, dvh = attend_backward(qkv, kv_halo, segs, lse, d_mixed)
    dkv = halo_back(jnp.concatenate([dkh, dvh], axis=1), jnp.concatenate([dk, dv], axis=1), *shift)
    dqkv = jnp.concatenate([dq, dkv.astype(BF)], axis=1)
    dw_qkv = mm_l(a1, dqkv)
    sums = column_sums(dqkv)
    du, dgain_attn = norm_backward(mm_t(dqkv, w_qkv), u, gain_attn)
    grads = (
        dgain_attn, dw_qkv, sums[:width], sums[2 * width :], dw_out, column_sums(dy),
        dgain_mlp, dw_up, column_sums(dz), dw_down, column_sums(dy2),
    )
    return g + du, grads


def to_runs(x, block_order, size):
    batch, rows, width = x.shape
    block = rows // 2
    x = x.reshape(batch, 2, size, block // size, width).transpose(2, 0, 1, 3, 4)
    x = lax.all_to_all(x, "ctx", 0, 0, tiled=True)
    x = x.transpose(1, 0, 2, 3, 4).reshape(batch, 2 * size, block // size, width)
    x = jnp.take(x, jnp.argsort(block_order), axis=1)
    x = x.reshape(size, 2 * batch, block // size, width)
    x = lax.all_to_all(x, "ctx", 0, 0, tiled=True)
    return x.transpose(1, 0, 2, 3).reshape(batch * rows, width)


def from_runs(x, block_order, size, batch):
    rows, width = x.shape[0] // batch, x.shape[1]
    block = rows // 2
    x = x.reshape(2 * batch, size, block // size, width).transpose(1, 0, 2, 3)
    x = lax.all_to_all(x, "ctx", 0, 0, tiled=True)
    x = x.reshape(batch, 2 * size, block // size, width)
    x = jnp.take(x, block_order, axis=1)
    x = x.reshape(batch, size, 2, block // size, width).transpose(1, 0, 2, 3, 4)
    x = lax.all_to_all(x, "ctx", 0, 0, tiled=True)
    return x.transpose(1, 2, 0, 3, 4).reshape(batch, rows, width)


def gather_weight(w):
    return lax.all_gather(w, "fsdp", axis=1, tiled=True)


def total_gradient(g):
    part = lax.psum_scatter(g.astype(BF), "fsdp", scatter_dimension=1, tiled=True)
    return lax.psum(part, "ctx").astype(F32)


def shards(block_input, cotangent, segment_ids, block_order, *weights):
    batch, _, rows, narrow = block_input.shape
    size = lax.axis_size("ctx")
    length = segment_ids.shape[2]
    run = batch * rows
    runs = length // run
    layers = weights[0].shape[0]
    longest = length // 4
    halo_steps = -(-longest // run)
    halo = halo_steps * run
    shift = (halo_steps, runs, size)
    index = lax.axis_index("ctx")
    own_seq = lax.dynamic_index_in_dim(segment_ids[:, 0], index // runs, 0, keepdims=False)
    padded = jnp.concatenate([jnp.full((halo,), -1, jnp.int32), own_seq])
    seg_window = lax.dynamic_slice_in_dim(padded, (index % runs) * run, halo + run)
    seg_halo, seg_own = seg_window[None, :halo], seg_window[None, halo:]
    segs = (seg_own.reshape(run, 1), seg_own, seg_halo)

    pad = [(0, 0), (0, 0), (0, 1)]
    both = jnp.concatenate([block_input[:, 0], cotangent[:, 0]], axis=2)
    both = jnp.pad(both, [(0, 0), (0, 0), (0, 2)])
    both = to_runs(both, block_order, size).astype(F32)
    h, ct = both[:, :narrow], both[:, narrow : 2 * narrow]
    u = jnp.concatenate([h, -jnp.sum(h, axis=1, keepdims=True)], axis=1)
    g = jnp.pad(ct, [(0, 0), (0, 1)])

    full = [gather_weight(w) for w in weights]
    per_layer = [
        tuple(w[layer] if w.ndim == 3 else w[layer].astype(F32) for w in full) for layer in range(layers)
    ]
    kept = []
    for layer in range(layers):
        u, saved = layer_forward(u, per_layer[layer], segs, shift)
        kept.append(saved)
    out = from_runs(u.astype(BF), block_order, size, batch)[:, None, :, :narrow]
    grads = [None] * layers
    for layer in reversed(range(layers)):
        g, grads[layer] = layer_backward(g, kept[layer], per_layer[layer], segs, shift)
    d_in = (g - g[:, narrow:]).astype(BF)
    d_in = from_runs(d_in, block_order, size, batch)[:, None, :, :narrow].astype(F32)
    totals = [total_gradient(jnp.stack([grads[layer][m] for layer in range(layers)])) for m in range(11)]
    return (out, d_in, *totals)


def solution(mesh):
    rows = P(None, "fsdp", "ctx", None)
    mat, vec = P(None, "fsdp", None), P(None, "fsdp")
    kinds = (vec, mat, vec, vec, mat, vec, vec, mat, vec, mat, vec)
    return jax.shard_map(
        shards,
        mesh=mesh,
        in_specs=(rows, rows, mat, P(), *kinds),
        out_specs=(rows, rows, *kinds),
        check_vma=False,
    )
```

time: 2590 us -> 1190 us (0.46)
  matrix products: 771 us -> 116 us
  waiting for transfers between devices: 1160 us -> 738 us
  local copies, waits for them, and re-layouts: 366 us -> 44 us
  Pallas kernels: 0 us -> 85.7 us
  other arithmetic: 130 us -> 56.1 us
  starting transfers between devices: 2.23 us -> 53.3 us
  loops' own time: 35.4 us -> 0 us
    dot_general x216 -> x24, matrix products: 771 us -> 116 us  [the longest x8 40 us: mm_t(): lax.dot_general(a, w, (((1,), (1,)), ((), ())), preferred_element_type=F32)]
    reduce_scatter x24 -> x4, waiting for transfers between devices: 702 us -> 185 us  [total_gradient(): lax.psum_scatter(g.astype(BF), 'fsdp', scatter_dimension=1, tiled=True)]
    all_gather x16 -> x4, waiting for transfers between devices: 341 us -> 165 us  [gather_weight(): return lax.all_gather(w, 'fsdp', axis=1, tiled=True)]
    dynamic_slice x216 -> x2, local copies, waits for them, and re-layouts: 170 us -> 0.08 us  [the longest x1 0.08 us: shards(): lax.dynamic_slice_in_dim(padded, index % runs * run, halo + run)]
    unnamed x41 -> x23, waiting for transfers between devices: 5.76 us -> 155 us
    pallas_call x0 -> x4, Pallas kernels: none -> 85.7 us  [the longest x2 52.6 us: attend_backward(): pl.pallas_call(attend_back_kernel, name='attend_backward', grid=(pairs,),...]
    all_to_all x0 -> x6, waiting for transfers between devices: none -> 69 us  [the longest x2 36.5 us: to_runs(): x = lax.all_to_all(x, 'ctx', 0, 0, tiled=True)]
    unnamed x447 -> x154, local copies, waits for them, and re-layouts: 80 us -> 29.4 us
  transfers between devices with their start and end apart: 41 -> 26, of which waited for: 28 -> 17; matrix products, arithmetic and copies ran while one was open for 32% -> 11% of each run, Pallas kernels for 0% -> 4%
where the time goes in v1:
time: 1190 us; the launch traced here: 1180 us
  waiting for transfers between devices  738 us (62%)
  matrix products  116 us (10%)
  Pallas kernels  85.7 us (7%)
  blocking collectives  70.7 us (6%)
  other arithmetic  56.1 us (5%)
  starting transfers between devices  53.3 us (4%)
  local copies, waits for them, and re-layouts  44 us (4%)
  between operations  15.5 us (1%)
    reduce_scatter x4, waiting for transfers between devices, total_gradient(): lax.psum_scatter(g.astype(BF), 'fsdp', scatter_dimension=1, tiled=True)  185 us
    all_gather x4, waiting for transfers between devices, gather_weight(): return lax.all_gather(w, 'fsdp', axis=1, tiled=True)  165 us
    unnamed x23, waiting for transfers between devices  155 us
    psum x1, waiting for transfers between devices, total_gradient(): return lax.psum(part, 'ctx').astype(F32)  128 us
    all_gather x7, blocking collectives, gather_weight(): return lax.all_gather(w, 'fsdp', axis=1, tiled=True)  53.7 us
    pallas_call x2, Pallas kernels, attend_backward(): pl.pallas_call(attend_back_kernel, name='attend_backward', grid=(pairs,),...  52.6 us
    dot_general x8, matrix products, mm_t(): lax.dot_general(a, w, (((1,), (1,)), ((), ())), preferred_element_type=F32)  40 us
    dot_general x8, matrix products, mm(): return jnp.dot(a, w, preferred_element_type=F32)  39.6 us
  transfers between devices with their start and end apart: 26, of which 17 were waited for; matrix products, arithmetic and copies ran while one was open for 11% of the time, Pallas kernels for 4%

profile of v1, /device:TPU:0, one launch (start us, length us, event | category | flops | bytes accessed | tf_op | source)
XLA Modules:
  0.0 1179.2 jit_solution(14165391794267376300)
XLA Ops:
  14.2 6.5 all-to-all-start
  22.0 36.5 %all-to-all-done = bf16[8,2,2,16,1536]{4,3,2,1,0:T(8,128)(2,1)S(1)} async-done(((bf16[8,2,2,16,1536]{4,3,2,1,0:T(8,128)(2,1)}), bf16[8,2,2,16,1536]{4,3,2,1,0:T(8,128)(2,1)S(1)}, u32[]{:S(2)}, u32[]{:S(2)}) %all-to-all-start) | async-done | bytes 1572896 | tf_op jit(solution)/shard_map/all_to_all | solution.py:286
  64.6 8.1 all-gather
  72.8 8.0 all-gather.1
  80.9 7.1 all-gather.2
  88.1 8.0 all-gather.3
  96.2 7.1 all-gather.4
  103.4 8.0 all-gather.5
  113.4 4.2 fusion.18.q_ref.k_ref.v_ref
  124.3 7.4 all_gather.41
  131.8 16.6 %attend_forward.2 = (bf16[512,768]{1,0:T(8,128)(2,1)}, f32[512,768]{1,0:T(8,128)}) custom-call(bf16[512,2304]{1,0:T(8,128)(2,1)} %copy-done.24, bf16[512,2304]{1,0:T(8,128)(2,1)} %copy-done.24, bf16[512,2304]{1,0:T(8,128)(2,1)} %copy-done.24, bf16[512,1536]{1,0:T(8,128)(2,1)} %collective-permute-done.kh_ref.vh_ref, ...), custom_call_target="tpu_custom_call" | custom-call | flops 1610612736 | bytes 4718592 | tf_op jit(solution)/shard_map/attend_forward/pallas_call | solution.py:77
  152.3 74.7 %all-gather.15.cloned.1.call-done = bf16[2,768,3072]{2,1,0:T(8,128)(2,1)} async-done(((bf16[2,192,3072]{2,1,0:T(8,128)(2,1)}), bf16[2,768,3072]{2,1,0:T(8,128)(2,1)}) %all-gather.15.cloned.1.call-update) | async-done | bytes 9437200 | tf_op jit(solution)/shard_map/all_gather | solution.py:307
  227.1 8.1 fusion.23
  235.2 90.0 %all-gather.17.cloned.1.call-done = bf16[2,3072,768]{2,1,0:T(8,128)(2,1)} async-done(((bf16[2,768,768]{2,1,0:T(8,128)(2,1)}), bf16[2,3072,768]{2,1,0:T(8,128)(2,1)}) %all-gather.17.cloned.1.call-update) | async-done | bytes 9437200 | tf_op jit(solution)/shard_map/all_gather | solution.py:307
  325.1 8.3 add_reduce_fusion.1
  333.9 4.6 fusion.19.q_ref.k_ref.v_ref
  343.6 16.5 %attend_forward.3 = (bf16[512,768]{1,0:T(8,128)(2,1)}, f32[512,768]{1,0:T(8,128)}) custom-call(bf16[512,2304]{1,0:T(8,128)(2,1)} %copy-done.25, bf16[512,2304]{1,0:T(8,128)(2,1)} %copy-done.25, bf16[512,2304]{1,0:T(8,128)(2,1)} %copy-done.25, bf16[512,1536]{1,0:T(8,128)(2,1)} %collective-permute-done.1.kh_ref.vh_ref, ...), custom_call_target="tpu_custom_call" | custom-call | flops 1610612736 | bytes 4718592 | tf_op jit(solution)/shard_map/attend_forward/pallas_call | solution.py:77
  363.1 5.3 fusion.27
  372.7 7.9 fusion.73
  380.6 4.8 multiply_reduce_fusion
  391.4 26.4 %attend_backward.2 = (bf16[512,768]{1,0:T(8,128)(2,1)}, f32[512,768]{1,0:T(8,128)}, f32[512,768]{1,0:T(8,128)}, bf16[512,768]{1,0:T(8,128)(2,1)}, bf16[512,768]{1,0:T(8,128)(2,1)}) custom-call(bf16[512,2304]{1,0:T(8,128)(2,1)} %copy-done.25, bf16[512,2304]{1,0:T(8,128)(2,1)} %copy-done.25, bf16[512,2304]{1,0:T(8,128)(2,1)} %copy-done.25, ...), custom_call_target="tpu_custom_call" | custom-call | flops 4026531840 | bytes 11796480 | tf_op jit(solution)/shard_map/attend_backward/pallas_call | solution.py:158
  421.8 18.6 %collective-permute-done.2 = bf16[512,1536]{1,0:T(8,128)(2,1)S(1)} collective-permute-done((bf16[512,1536]{1,0:T(8,128)(2,1)S(1)}, bf16[512,1536]{1,0:T(8,128)(2,1)S(1)}, u32[]{:S(2)}, u32[]{:S(2)}) %collective-permute-start.2) | collective-permute-done | bytes 1572896 | tf_op jit(solution)/shard_map/ppermute | solution.py:222
  442.6 5.0 multiply_reduce_fusion.2
  449.0 7.8 fusion.74
  456.8 4.8 multiply_reduce_fusion.1
  469.1 26.3 %attend_backward.3 = (bf16[512,768]{1,0:T(8,128)(2,1)}, f32[512,768]{1,0:T(8,128)}, f32[512,768]{1,0:T(8,128)}, bf16[512,768]{1,0:T(8,128)(2,1)}, bf16[512,768]{1,0:T(8,128)(2,1)}) custom-call(bf16[512,2304]{1,0:T(8,128)(2,1)} %copy-done.24, bf16[512,2304]{1,0:T(8,128)(2,1)} %copy-done.24, bf16[512,2304]{1,0:T(8,128)(2,1)} %copy-done.24, ...), custom_call_target="tpu_custom_call" | custom-call | flops 4026531840 | bytes 11796480 | tf_op jit(solution)/shard_map/attend_backward/pallas_call | solution.py:158
  502.3 17.6 %collective-permute-done.3 = bf16[512,1536]{1,0:T(8,128)(2,1)S(1)} collective-permute-done((bf16[512,1536]{1,0:T(8,128)(2,1)S(1)}, bf16[512,1536]{1,0:T(8,128)(2,1)S(1)}, u32[]{:S(2)}, u32[]{:S(2)}) %collective-permute-start.3) | collective-permute-done | bytes 1572896 | tf_op jit(solution)/shard_map/ppermute | solution.py:222
  527.1 8.9 fusion.17
  536.0 8.7 fusion.16
  544.7 8.3 pad_maximum_fusion.1
  553.2 7.4 fusion.15
  560.7 4.5 fusion.14
  565.1 8.7 pad_maximum_fusion
  576.7 20.8 %all-to-all-start.2 = ((bf16[8,4,16,768]{3,2,1,0:T(8,128)(2,1)}), bf16[8,4,16,768]{3,2,1,0:T(8,128)(2,1)}, u32[]{:S(2)}, u32[]{:S(2)}) async-start(bf16[8,4,16,768]{3,2,1,0:T(8,128)(2,1)} %bitcast.199), calls=%async_computation.2 | async-start | bytes 1572864 | tf_op jit(solution)/shard_map/all_to_all | solution.py:298
  599.4 4.9 multiply_reduce_fusion.3
  606.2 12.6 %all-to-all-done.2 = bf16[8,4,16,768]{3,2,1,0:T(8,128)(2,1)} async-done(((bf16[8,4,16,768]{3,2,1,0:T(8,128)(2,1)}), bf16[8,4,16,768]{3,2,1,0:T(8,128)(2,1)}, u32[]{:S(2)}, u32[]{:S(2)}) %all-to-all-start.2) | async-done | bytes 786464 | tf_op jit(solution)/shard_map/all_to_all | solution.py:298
  631.4 86.4 %reduce-scatter.32.cloned.1.call-done = bf16[2,768,768]{2,1,0:T(8,128)(2,1)} async-done(((bf16[2,3072,768]{2,1,0:T(8,128)(2,1)}), bf16[2,768,768]{2,1,0:T(8,128)(2,1)}) %reduce-scatter.32.cloned.1.call-update) | async-done | bytes 2359312 | tf_op jit(solution)/shard_map/reduce_scatter | solution.py:311
  717.8 98.2 %reduce-scatter.30.cloned.1.call-done = bf16[2,192,3072]{2,1,0:T(8,128)(2,1)} async-done(((bf16[2,768,3072]{2,1,0:T(8,128)(2,1)}), bf16[2,192,3072]{2,1,0:T(8,128)(2,1)}) %reduce-scatter.30.cloned.1.call-update) | async-done | bytes 2359312 | tf_op jit(solution)/shard_map/reduce_scatter | solution.py:311
  820.6 4.6 all-to-all-start.3
  826.2 20.0 %all-to-all-done.3 = bf16[8,2,2,16,768]{4,3,2,1,0:T(8,128)(2,1)S(1)} async-done(((bf16[8,2,2,16,768]{4,3,2,1,0:T(8,128)(2,1)}), bf16[8,2,2,16,768]{4,3,2,1,0:T(8,128)(2,1)S(1)}, u32[]{:S(2)}, u32[]{:S(2)}) %all-to-all-start.3) | async-done | bytes 786464 | tf_op jit(solution)/shard_map/all_to_all | solution.py:302
  850.7 18.6 %reduce-scatter.42.cloned.1.call-done = bf16[192,2]{1,0:T(8,128)(2,1)} async-done(((bf16[768,2]{1,0:T(8,128)(2,1)}), bf16[192,2]{1,0:T(8,128)(2,1)}) %reduce-scatter.42.cloned.1.call-update) | async-done | bytes 784
  870.2 25.9 %reduce-scatter.40.cloned.1.call-done = bf16[192,2]{1,0:T(8,128)(2,1)} async-done(((bf16[768,2]{1,0:T(8,128)(2,1)}), bf16[192,2]{1,0:T(8,128)(2,1)}) %reduce-scatter.40.cloned.1.call-update) | async-done | bytes 784
  897.0 28.6 %reduce-scatter.44.cloned.1.call-done = bf16[768,2]{1,0:T(8,128)(2,1)} async-done(((bf16[3072,2]{1,0:T(8,128)(2,1)}), bf16[768,2]{1,0:T(8,128)(2,1)}) %reduce-scatter.44.cloned.1.call-update) | async-done | bytes 3088
  926.6 26.3 %reduce-scatter.36.cloned.1.call-done = bf16[192,2]{1,0:T(8,128)(2,1)} async-done(((bf16[768,2]{1,0:T(8,128)(2,1)}), bf16[192,2]{1,0:T(8,128)(2,1)}) %reduce-scatter.36.cloned.1.call-update) | async-done | bytes 784
  953.8 26.3 %reduce-scatter.38.cloned.1.call-done = bf16[192,2]{1,0:T(8,128)(2,1)} async-done(((bf16[768,2]{1,0:T(8,128)(2,1)}), bf16[192,2]{1,0:T(8,128)(2,1)}) %reduce-scatter.38.cloned.1.call-update) | async-done | bytes 784
  981.0 26.3 %reduce-scatter.34.cloned.1.call-done = bf16[192,2]{1,0:T(8,128)(2,1)} async-done(((bf16[768,2]{1,0:T(8,128)(2,1)}), bf16[192,2]{1,0:T(8,128)(2,1)}) %reduce-scatter.34.cloned.1.call-update) | async-done | bytes 784
  1008.2 16.9 %all-reduce.3 = (bf16[2,192]{1,0:T(2,128)(2,1)S(1)}, bf16[2,192]{1,0:T(2,128)(2,1)S(1)}, bf16[2,192]{1,0:T(2,128)(2,1)S(1)}, bf16[2,192]{1,0:T(2,128)(2,1)S(1)},...) all-reduce(bf16[2,192]{1,0:T(2,128)(2,1)S(1)} %copy.83, ...), channel_id=1, replica_groups=mesh['ctx'=8,'fsdp'=4] {'ctx'}, use_global_device_ids=true, to_apply=%region_21.23 | all-reduce | flops 3840 | bytes 15360 | tf_op jit(solution)/shard_map/psum | solution.py:312
  1034.0 128.0 %all-reduce.7.cloned.1.call-done = (bf16[2,192,2304]{2,1,0:T(8,128)(2,1)}, bf16[2,192,768]{2,1,0:T(8,128)(2,1)}, bf16[2,192,3072]{2,1,0:T(8,128)(2,1)}, bf16[2,768,768]{2,1,0:T(8,128)(2,1)}) async-done(((bf16[2,192,2304]{2,1,0:T(8,128)(2,1)}, bf16[2,192,768]{2,1,0:T(8,128)(2,1)}, bf16[2,192,3072]{2,1,0:T(8,128)(2,1)}, bf16[2,768,768]{2,1,0:T(8,128)(2,1)}), (bf16[2,192,2304]{2,1,0:T(8,128)(2,1)}, ...) | async-done | bytes 7077904 | tf_op jit(solution)/shard_map/psum | solution.py:312
  (342 shorter events, 128.7 us)
Async XLA Ops:
  7.2 115.6 %copy-start = (s32[2,1,2048]{2,1,0:T(1,128)S(1)}, s32[2,1,2048]{2,1,0:T(1,128)}, u32[]{:S(2)}) copy-start(s32[2,1,2048]{2,1,0:T(1,128)} %param.19) | copy-start | bytes 49156
  7.2 106.2 %all-gather.11.cloned.1.call-start = ((), (), s32[]{:S(2)}) async-start(), calls=%async_computation.17 | async-start | bytes 8847360 | tf_op jit(solution)/shard_map/all_gather | solution.py:307
  7.9 140.4 %all-gather.13.cloned.1.call-start = ((), (), s32[]{:S(2)}) async-start(), calls=%async_computation.18 | async-start | bytes 2949120 | tf_op jit(solution)/shard_map/all_gather | solution.py:307
  8.7 218.4 %all-gather.15.cloned.1.call-start = ((), (), s32[]{:S(2)}) async-start(), calls=%async_computation.19 | async-start | bytes 11796480 | tf_op jit(solution)/shard_map/all_gather | solution.py:307
  9.4 315.7 %all-gather.17.cloned.1.call-start = ((), (), s32[]{:S(2)}) async-start(), calls=%async_computation.20 | async-start | bytes 11796480 | tf_op jit(solution)/shard_map/all_gather | solution.py:307
  14.2 44.3 %all-to-all-start = ((bf16[8,2,2,16,1536]{4,3,2,1,0:T(8,128)(2,1)}), bf16[8,2,2,16,1536]{4,3,2,1,0:T(8,128)(2,1)S(1)}, u32[]{:S(2)}, u32[]{:S(2)}) async-start(bf16[8,2,2,16,1536]{4,3,2,1,0:T(8,128)(2,1)} %copy.55), calls=%async_computation | async-start | bytes 3145728 | tf_op jit(solution)/shard_map/all_to_all | solution.py:286
  60.7 12.0 %copy-start.39 = (bf16[2,192]{1,0:T(2,128)(2,1)S(1)}, bf16[2,192]{1,0:T(2,128)(2,1)}, u32[]{:S(2)}) copy-start(bf16[2,192]{1,0:T(2,128)(2,1)} %param.23) | copy-start | bytes 2308
  60.7 20.2 %copy-start.40 = (bf16[2,192]{1,0:T(2,128)(2,1)S(1)}, bf16[2,192]{1,0:T(2,128)(2,1)}, u32[]{:S(2)}) copy-start(bf16[2,192]{1,0:T(2,128)(2,1)} %param.24) | copy-start | bytes 2308
  60.7 27.4 %copy-start.41 = (bf16[2,192]{1,0:T(2,128)(2,1)S(1)}, bf16[2,192]{1,0:T(2,128)(2,1)}, u32[]{:S(2)}) copy-start(bf16[2,192]{1,0:T(2,128)(2,1)} %param.26) | copy-start | bytes 2308
  60.7 35.5 %copy-start.42 = (bf16[2,192]{1,0:T(2,128)(2,1)S(1)}, bf16[2,192]{1,0:T(2,128)(2,1)}, u32[]{:S(2)}) copy-start(bf16[2,192]{1,0:T(2,128)(2,1)} %param.27) | copy-start | bytes 2308
  60.8 42.6 %copy-start.43 = (bf16[2,192]{1,0:T(2,128)(2,1)S(1)}, bf16[2,192]{1,0:T(2,128)(2,1)}, u32[]{:S(2)}) copy-start(bf16[2,192]{1,0:T(2,128)(2,1)} %param.31) | copy-start | bytes 2308
  60.8 50.9 %all-to-all-start.1 = ((bf16[8,4,16,1536]{3,2,1,0:T(8,128)(2,1)}), bf16[8,4,16,1536]{3,2,1,0:T(8,128)(2,1)S(1)}, u32[]{:S(2)}, u32[]{:S(2)}) async-start(bf16[8,4,16,1536]{3,2,1,0:T(8,128)(2,1)} %broadcast_select_fusion), calls=%async_computation.1 | async-start | bytes 3145728 | tf_op jit(solution)/shard_map/all_to_all | solution.py:290
  64.5 566.9 %reduce-scatter.28.cloned.1.call-start = ((), (), s32[]{:S(2)}) async-start(), calls=%async_computation.22 | async-start | bytes 2949120 | tf_op jit(solution)/shard_map/reduce_scatter | solution.py:311
  120.3 11.4 collective-permute-start
  123.4 8.4 copy-start.36
  325.1 8.3 copy-start.2
  338.7 4.9 collective-permute-start.1
  360.1 8.4 slice-start.6
  363.1 22.3 %copy-start.16 = (f32[512,768]{1,0:T(8,128)}, f32[512,768]{1,0:T(8,128)S(1)}, u32[]{:S(2)}) copy-start(f32[512,768]{1,0:T(8,128)S(1)} %get-tuple-element.116) | copy-start | bytes 4718596
  368.5 12.1 %slice-start = ((s8[9437184]{0:T(1024)(128)(4,1)}), s8[4194304]{0:T(1024)(128)(4,1)S(1)}, s32[]{:S(2)}) async-start(s8[9437184]{0:T(1024)(128)(4,1)} %bitcast.250), calls=%async_computation.33 | async-start | bytes 8388608
  368.5 12.1 %slice-start.1 = ((s8[9437184]{0:T(1024)(128)(4,1)}), s8[4194304]{0:T(1024)(128)(4,1)S(1)}, s32[]{:S(2)}) async-start(s8[9437184]{0:T(1024)(128)(4,1)} %bitcast.250), calls=%async_computation.34 | async-start | bytes 8388608
  387.4 30.4 %copy-start.31 = (bf16[512,768]{1,0:T(8,128)(2,1)}, bf16[512,768]{1,0:T(8,128)(2,1)S(1)}, u32[]{:S(2)}) copy-start(bf16[512,768]{1,0:T(8,128)(2,1)S(1)} %get-tuple-element.108) | copy-start | bytes 2359300
  419.4 21.0 %copy-start.22 = (f32[512,768]{1,0:T(8,128)S(1)}, f32[512,768]{1,0:T(8,128)}, u32[]{:S(2)}) copy-start(f32[512,768]{1,0:T(8,128)} %get-tuple-element.34) | copy-start | bytes 4718596
  419.4 21.0 %copy-start.23 = (f32[512,768]{1,0:T(8,128)S(1)}, f32[512,768]{1,0:T(8,128)}, u32[]{:S(2)}) copy-start(f32[512,768]{1,0:T(8,128)} %get-tuple-element.35) | copy-start | bytes 4718596
  419.4 21.0 %collective-permute-start.2 = (bf16[512,1536]{1,0:T(8,128)(2,1)S(1)}, bf16[512,1536]{1,0:T(8,128)(2,1)S(1)}, u32[]{:S(2)}, u32[]{:S(2)}) collective-permute-start(bf16[512,1536]{1,0:T(8,128)(2,1)S(1)} %pad_maximum_fusion.7), channel_id=1, source_target_pairs={{4,0},{8,4},{12,8},{20,16},{24,20},{28,24},{5,1},{9,5},{13,9},{21,... | collective-permute-start | bytes 4718600 | tf_op jit(solution)/shard_map/ppermute | solution.py:222
  440.5 8.2 slice-start.9
  440.5 8.2 slice-start.12
  447.7 9.1 slice-start.3
  465.9 165.5 %reduce-scatter.26.cloned.1.call-start = ((), (), s32[]{:S(2)}) async-start(), calls=%async_computation.21 | async-start | bytes 8847360 | tf_op jit(solution)/shard_map/reduce_scatter | solution.py:311
  497.1 22.9 %copy-start.20 = (f32[512,768]{1,0:T(8,128)S(1)}, f32[512,768]{1,0:T(8,128)}, u32[]{:S(2)}) copy-start(f32[512,768]{1,0:T(8,128)} %get-tuple-element.40) | copy-start | bytes 4718596
  497.1 22.9 %copy-start.21 = (f32[512,768]{1,0:T(8,128)S(1)}, f32[512,768]{1,0:T(8,128)}, u32[]{:S(2)}) copy-start(f32[512,768]{1,0:T(8,128)} %get-tuple-element.41) | copy-start | bytes 4718596
  497.1 22.8 %collective-permute-start.3 = (bf16[512,1536]{1,0:T(8,128)(2,1)S(1)}, bf16[512,1536]{1,0:T(8,128)(2,1)S(1)}, u32[]{:S(2)}, u32[]{:S(2)}) collective-permute-start(bf16[512,1536]{1,0:T(8,128)(2,1)S(1)} %pad_maximum_fusion.8), channel_id=1, source_target_pairs={{4,0},{8,4},{12,8},{20,16},{24,20},{28,24},{5,1},{9,5},{13,9},{21,... | collective-permute-start | bytes 4718600 | tf_op jit(solution)/shard_map/ppermute | solution.py:222
  527.0 190.7 %reduce-scatter.32.cloned.1.call-start = ((), (), s32[]{:S(2)}) async-start(), calls=%async_computation.24 | async-start | bytes 11796480 | tf_op jit(solution)/shard_map/reduce_scatter | solution.py:311
  527.1 9.0 copy-start.30
  553.0 263.0 %reduce-scatter.30.cloned.1.call-start = ((), (), s32[]{:S(2)}) async-start(), calls=%async_computation.23 | async-start | bytes 11796480 | tf_op jit(solution)/shard_map/reduce_scatter | solution.py:311
  576.7 42.1 %all-to-all-start.2 = ((bf16[8,4,16,768]{3,2,1,0:T(8,128)(2,1)}), bf16[8,4,16,768]{3,2,1,0:T(8,128)(2,1)}, u32[]{:S(2)}, u32[]{:S(2)}) async-start(bf16[8,4,16,768]{3,2,1,0:T(8,128)(2,1)} %bitcast.199), calls=%async_computation.2 | async-start | bytes 1572864 | tf_op jit(solution)/shard_map/all_to_all | solution.py:298
  597.5 252.3 %reduce-scatter.46.cloned.1.call-start = ((), (), s32[]{:S(2)}) async-start(), calls=%async_computation.31 | async-start | bytes 245760
  598.5 270.8 %reduce-scatter.42.cloned.1.call-start = ((), (), s32[]{:S(2)}) async-start(), calls=%async_computation.29 | async-start | bytes 245760
  605.2 18.8 %copy-start.13 = (bf16[512,1536]{1,0:T(8,128)(2,1)S(1)}, bf16[512,1536]{1,0:T(8,128)(2,1)}, u32[]{:S(2)}) copy-start(bf16[512,1536]{1,0:T(8,128)(2,1)} %copy-done.11) | copy-start | bytes 4718596
  618.7 199.0 %all-to-all-start.4 = ((bf16[8,4,16,768]{3,2,1,0:T(8,128)(2,1)}), bf16[8,4,16,768]{3,2,1,0:T(8,128)(2,1)}, u32[]{:S(2)}, u32[]{:S(2)}) async-start(bf16[8,4,16,768]{3,2,1,0:T(8,128)(2,1)} %bitcast.190), calls=%async_computation.4 | async-start | bytes 1572864 | tf_op jit(solution)/shard_map/all_to_all | solution.py:298
  623.0 273.2 %reduce-scatter.40.cloned.1.call-start = ((), (), s32[]{:S(2)}) async-start(), calls=%async_computation.28 | async-start | bytes 245760
  623.9 301.7 %reduce-scatter.44.cloned.1.call-start = ((), (), s32[]{:S(2)}) async-start(), calls=%async_computation.30 | async-start | bytes 983040
  626.8 326.1 %reduce-scatter.36.cloned.1.call-start = ((), (), s32[]{:S(2)}) async-start(), calls=%async_computation.26 | async-start | bytes 245760
  629.4 350.7 %reduce-scatter.38.cloned.1.call-start = ((), (), s32[]{:S(2)}) async-start(), calls=%async_computation.27 | async-start | bytes 245760
  630.3 376.9 %reduce-scatter.34.cloned.1.call-start = ((), (), s32[]{:S(2)}) async-start(), calls=%async_computation.25 | async-start | bytes 245760
  631.3 530.7 %all-reduce.7.cloned.1.call-start = ((), (), s32[]{:S(2)}) async-start(), calls=%async_computation.32 | async-start | bytes 14155776 | tf_op jit(solution)/shard_map/psum | solution.py:312
  820.6 25.6 %all-to-all-start.3 = ((bf16[8,2,2,16,768]{4,3,2,1,0:T(8,128)(2,1)}), bf16[8,2,2,16,768]{4,3,2,1,0:T(8,128)(2,1)S(1)}, u32[]{:S(2)}, u32[]{:S(2)}) async-start(bf16[8,2,2,16,768]{4,3,2,1,0:T(8,128)(2,1)} %copy.70), calls=%async_computation.3 | async-start | bytes 1572864 | tf_op jit(solution)/shard_map/all_to_all | solution.py:302
  846.2 184.9 %all-to-all-start.5 = ((bf16[8,2,2,16,768]{4,3,2,1,0:T(8,128)(2,1)}), bf16[8,2,2,16,768]{4,3,2,1,0:T(8,128)(2,1)S(1)}, u32[]{:S(2)}, u32[]{:S(2)}) async-start(bf16[8,2,2,16,768]{4,3,2,1,0:T(8,128)(2,1)} %copy.76), calls=%async_computation.5 | async-start | bytes 1572864 | tf_op jit(solution)/shard_map/all_to_all | solution.py:302
  (43 other events, 178.4 us)
Sparse Core Ops, SparseCore 0:
  9.9 79.5 all-gather.10
  91.3 37.4 all-gather.12
  130.6 96.3 all-gather.14
  228.8 96.3 all-gather.16
  466.0 53.9 reduce-scatter.27
  527.1 92.4 reduce-scatter.25
  622.7 94.9 reduce-scatter.31
  720.9 95.0 reduce-scatter.29
  818.7 23.9 reduce-scatter.45
  845.3 23.9 reduce-scatter.41
  872.1 23.9 reduce-scatter.39
  899.4 26.0 reduce-scatter.43
  928.9 23.9 reduce-scatter.35
  956.1 23.9 reduce-scatter.37
  983.3 23.9 reduce-scatter.33
  1009.8 152.1 all-reduce.6
